TPU v7x, 128 devices: a whole 4x4x4 slice. The times are simulated.
128 devices in a mesh: wide: 16 (over y, z_hi, core), narrow: 8 (over z_lo, x).
Axes of the slice: x: 4, y: 4, z: 4 (z_hi: 2, z_lo: 2; z = z_hi * 2 + z_lo), core: 2. Of those that a mesh axis runs over, the one named last changes fastest.
Arguments:
- pressure: float32 [64, 512, 512], P('wide', 'narrow'), may hold values from -6 to 6
- source: float32 [64, 512, 512], P('wide', 'narrow'), may hold values from -6 to 6
- permeability: float32 [64, 512, 512], P('wide', 'narrow'), may hold values from 0.1 to 10
- active_mask: int32 [64, 512, 512], P('wide', 'narrow'), may hold values 0 or 1
Outputs:
- smoothed_pressure: float32 [64, 512, 512], P('wide', 'narrow')
Inputs may be any that keep to these rules, and one draw needn't show every extreme that they name: `active_mask`: 1 marks an active cell.
All inputs are finite; a program needn't handle non-finite values. No bound on the sum of `active_mask` on one device may be relied on, other than what follows from the above.
Results may differ from a plain program's by a relative error of at most 0.00002.
Values sent between devices are 32-bit elements; how exact they have to be, the bound alone decides.
A program may use at most 256 MiB of HBM per device.

v0:
```python
import jax
import jax.numpy as jnp
from jax import lax
from jax.sharding import PartitionSpec as P

RELAX_WEIGHT = 0.8
STORE_COEFF = 0.5
FLOOR_SUM = 0.1
NEIGHBOURS = ((0, 1, 1), (2, 1, 1), (1, 0, 1), (1, 2, 1), (1, 1, 0), (1, 1, 2))


def extended(block, sides, width):
    for axis, dim in sides:
        count = lax.axis_size(axis)
        forward = [(i, i + 1) for i in range(count - 1)]
        backward = [(target, source) for source, target in forward]
        low = lax.ppermute(
            lax.slice_in_dim(block, block.shape[dim] - width, None, axis=dim), axis, forward
        )
        high = lax.ppermute(lax.slice_in_dim(block, 0, width, axis=dim), axis, backward)
        block = jnp.concatenate([low, block, high], axis=dim)
    return block


def relax_cells(padded_field, padded_perm, source, active, spacing):
    size_x, size_z, size_y = source.shape
    field_pad = jnp.pad(padded_field, ((0, 0), (0, 0), (1, 1)))
    perm_pad = jnp.pad(padded_perm, ((0, 0), (0, 0), (1, 1)))
    centre_field = field_pad[1 : size_x + 1, 1 : size_z + 1, 1 : size_y + 1]
    centre_perm = perm_pad[1 : size_x + 1, 1 : size_z + 1, 1 : size_y + 1]
    flux_sum = jnp.zeros(source.shape, jnp.float32)
    weight = jnp.zeros(source.shape, jnp.float32)
    for off_x, off_z, off_y in NEIGHBOURS:
        near_field = field_pad[
            off_x : off_x + size_x, off_z : off_z + size_z, off_y : off_y + size_y
        ]
        near_perm = perm_pad[off_x : off_x + size_x, off_z : off_z + size_z, off_y : off_y + size_y]
        conduct = 2.0 * centre_perm * near_perm / jnp.maximum(centre_perm + near_perm, FLOOR_SUM)
        flux_sum = flux_sum + conduct * (centre_field - near_field)
        weight = weight + conduct
    storage = STORE_COEFF * spacing**3
    residual = active * (source - storage * centre_field - spacing * flux_sum)
    updated = active * (centre_field + RELAX_WEIGHT * residual / (storage + spacing * weight))
    return (updated, residual)


def pad_plane(values):
    return jnp.pad(values, ((1, 1), (1, 1), (0, 0)))


def coarsen_sum(values):
    size_x, size_z, size_y = values.shape
    return values.reshape(size_x // 2, 2, size_z // 2, 2, size_y // 2, 2).sum(axis=(1, 3, 5))


def coarsen_max(values):
    size_x, size_z, size_y = values.shape
    return values.reshape(size_x // 2, 2, size_z // 2, 2, size_y // 2, 2).max(axis=(1, 3, 5))


def refine(values):
    return jnp.repeat(jnp.repeat(jnp.repeat(values, 2, 0), 2, 1), 2, 2)


def fine_halo(values):
    return extended(values, (("wide", 0), ("narrow", 1)), 1)


def mid_halo(values):
    return extended(values, (("wide", 0), ("narrow", 1)), 1)


def per_device(pressure, source, permeability, active_mask):
    fine_active = active_mask.astype(jnp.float32)
    fine_perm = permeability * fine_active
    fine_padm = extended(fine_perm, (("wide", 0), ("narrow", 1)), 1)
    fine_field = pressure
    for sweep_index in range(2):
        fine_field, unused = relax_cells(fine_halo(fine_field), fine_padm, source, fine_active, 1.0)
    unused, fine_resid = relax_cells(fine_halo(fine_field), fine_padm, source, fine_active, 1.0)
    mid_active = coarsen_max(fine_active)
    mid_raw = coarsen_sum(permeability) * 0.125
    mid_perm = mid_raw * mid_active
    mid_source = mid_active * coarsen_sum(fine_resid)
    mid_padm = extended(mid_perm, (("wide", 0), ("narrow", 1)), 1)
    mid_field = jnp.zeros(mid_source.shape, jnp.float32)
    mid_field, unused = relax_cells(pad_plane(mid_field), mid_padm, mid_source, mid_active, 2.0)
    mid_field, unused = relax_cells(mid_halo(mid_field), mid_padm, mid_source, mid_active, 2.0)
    unused, mid_resid = relax_cells(mid_halo(mid_field), mid_padm, mid_source, mid_active, 2.0)
    coarse_active = coarsen_max(mid_active)
    coarse_perm = coarsen_sum(mid_raw) * 0.125 * coarse_active
    coarse_source = coarse_active * coarsen_sum(mid_resid)
    coarse_padm = extended(coarse_perm, (("wide", 0), ("narrow", 1)), 1)
    coarse_field = jnp.zeros(coarse_source.shape, jnp.float32)
    coarse_field, unused = relax_cells(
        pad_plane(coarse_field), coarse_padm, coarse_source, coarse_active, 4.0
    )
    for sweep_index in range(3):
        padded = extended(coarse_field, (("wide", 0), ("narrow", 1)), 1)
        coarse_field, unused = relax_cells(padded, coarse_padm, coarse_source, coarse_active, 4.0)
    mid_field = mid_field + mid_active * refine(coarse_field)
    mid_field, unused = relax_cells(mid_halo(mid_field), mid_padm, mid_source, mid_active, 2.0)
    fine_field = fine_field + fine_active * refine(mid_field)
    fine_field, unused = relax_cells(fine_halo(fine_field), fine_padm, source, fine_active, 1.0)
    return fine_field


def solution(mesh):
    placed = (
        P("wide", "narrow", None),
        P("wide", "narrow", None),
        P("wide", "narrow", None),
        P("wide", "narrow", None),
    )
    return jax.shard_map(
        per_device, mesh=mesh, in_specs=placed, out_specs=P("wide", "narrow", None), check_vma=False
    )
```

profile of v0, /device:TPU:23, one launch (start us, length us, event | category | flops | bytes accessed | tf_op | source)
XLA Modules:
  0.0 456.8 jit_solution(2528226866598627370)
XLA Ops:
  2.8 6.1 %collective-permute-start = (f32[1,64,512]{2,1,0:T(8,128)}, f32[1,64,512]{2,1,0:T(8,128)S(1)}, u32[]{:S(2)}, u32[]{:S(2)}) collective-permute-start(f32[1,64,512]{2,1,0:T(8,128)} %get-tuple-element.40), channel_id=1, source_target_pairs={{0,8},{8,16},{16,24},{24,32},{32,40},{40,48},{48,56},{56,64},{64,7... | collective-permute-start | bytes 393224 | tf_op jit(solution)/shard_map/ppermute | solution.py:17
  10.8 5.1 %collective-permute-start.1 = (f32[1,64,512]{2,1,0:T(8,128)S(1)}, f32[1,64,512]{2,1,0:T(8,128)S(1)}, u32[]{:S(2)}, u32[]{:S(2)}) collective-permute-start(f32[1,64,512]{2,1,0:T(8,128)S(1)} %get-tuple-element.42), channel_id=1, source_target_pairs={{0,8},{8,16},{16,24},{24,32},{32,40},{40,48},{48,56},{56,64},{64,7... | collective-permute-start | bytes 393224 | tf_op jit(solution)/shard_map/ppermute | solution.py:17
  18.0 34.8 %reshape.82 = f32[2,2,32,2,256,2]{5,4,3,2,1,0:T(8,128)} reshape(f32[4,64,512]{2,1,0:T(8,128)S(1)} %copy-done.4) | data formatting | bytes 1048576 | tf_op jit(solution)/shard_map/reshape | solution.py:53
  52.8 34.8 %reshape.80 = f32[2,2,32,2,256,2]{5,4,3,2,1,0:T(8,128)} reshape(f32[4,64,512]{2,1,0:T(8,128)S(1)} %convert_element_type.34) | data formatting | bytes 1048576 | tf_op jit(solution)/shard_map/reshape | solution.py:58
  87.6 12.2 %reduce_max.24 = f32[2,32,256]{2,1,0:T(8,128)S(1)} reduce(f32[2,2,32,2,256,2]{5,4,3,2,1,0:T(8,128)} %reshape.80, f32[]{:T(128)} %constant.14.clone.1), dimensions={1,3,5}, to_apply=%region_0.1 | reduce | flops 114688 | bytes 589828 | tf_op jit(solution)/shard_map/reduce_max | solution.py:58
  99.9 12.9 %reduce_sum.44 = f32[2,32,256]{2,1,0:T(8,128)} reduce(f32[2,2,32,2,256,2]{5,4,3,2,1,0:T(8,128)} %reshape.82, f32[]{:T(128)} %constant.12.clone.1), dimensions={1,3,5}, to_apply=%region_2.3 | reduce | flops 114688 | bytes 589828 | tf_op jit(solution)/shard_map/reduce_sum | solution.py:53
  118.2 4.7 %collective-permute-start.5 = (f32[6,1,512]{2,1,0:T(1,128)S(1)}, f32[6,1,512]{2,1,0:T(1,128)S(1)}, u32[]{:S(2)}, u32[]{:S(2)}) collective-permute-start(f32[6,1,512]{2,1,0:T(1,128)S(1)} %get-tuple-element.29), channel_id=1, source_target_pairs={{0,1},{1,2},{2,3},{3,4},{4,5},{5,6},{6,7},{8,9},{9,10},{10,11},{11... | collective-permute-start | bytes 36872 | tf_op jit(solution)/shard_map/ppermute | solution.py:17
  125.4 4.1 collective-permute-done.7
  131.8 7.7 %collective-permute-start.8 = (f32[1,64,512]{2,1,0:T(8,128)S(1)}, f32[1,64,512]{2,1,0:T(8,128)S(1)}, u32[]{:S(2)}, u32[]{:S(2)}) collective-permute-start(f32[1,64,512]{2,1,0:T(8,128)S(1)} %get-tuple-element.37), channel_id=1, source_target_pairs={{0,8},{8,16},{16,24},{24,32},{32,40},{40,48},{48,56},{56,64},{64,7... | collective-permute-start | bytes 393224 | tf_op jit(solution)/shard_map/ppermute | solution.py:17
  142.1 5.2 %collective-permute-done.9 = f32[1,64,512]{2,1,0:T(8,128)S(1)} collective-permute-done((f32[1,64,512]{2,1,0:T(8,128)S(1)}, f32[1,64,512]{2,1,0:T(8,128)S(1)}, u32[]{:S(2)}, u32[]{:S(2)}) %collective-permute-start.9) | collective-permute-done | bytes 131104 | tf_op jit(solution)/shard_map/ppermute | solution.py:20
  160.2 5.1 %collective-permute-start.12 = (f32[1,64,512]{2,1,0:T(8,128)}, f32[1,64,512]{2,1,0:T(8,128)}, u32[]{:S(2)}, u32[]{:S(2)}) collective-permute-start(f32[1,64,512]{2,1,0:T(8,128)} %get-tuple-element.35), channel_id=1, source_target_pairs={{0,8},{8,16},{16,24},{24,32},{32,40},{40,48},{48,56},{56,64},{64,7... | collective-permute-start | bytes 393224 | tf_op jit(solution)/shard_map/ppermute | solution.py:17
  169.1 4.2 reduce_sum.59
  175.8 10.5 %reduce_max.29 = f32[32,2,256,2]{3,2,1,0:T(8,128)} reshape(f32[64,512]{1,0:T(8,128)} %get-tuple-element.33) | data formatting | bytes 262144 | tf_op jit(solution)/shard_map/reduce_max | solution.py:58
  186.3 5.1 %reduce_max.30 = f32[32,256]{1,0:T(8,128)} reduce(f32[32,2,256,2]{3,2,1,0:T(8,128)} %reduce_max.29, f32[]{:T(128)} %constant.14.clone.1), dimensions={1,3}, to_apply=%region_4.5 | reduce | flops 24576 | bytes 163844 | tf_op jit(solution)/shard_map/reduce_max | solution.py:58
  191.4 4.2 reduce_max.38
  205.4 5.5 %collective-permute-start.14 = (f32[6,1,512]{2,1,0:T(1,128)S(1)}, f32[6,1,512]{2,1,0:T(1,128)S(1)}, u32[]{:S(2)}, u32[]{:S(2)}) collective-permute-start(f32[6,1,512]{2,1,0:T(1,128)S(1)} %get-tuple-element.23), channel_id=1, source_target_pairs={{0,1},{1,2},{2,3},{3,4},{4,5},{5,6},{6,7},{8,9},{9,10},{10,11},{11... | collective-permute-start | bytes 36872 | tf_op jit(solution)/shard_map/ppermute | solution.py:17
  221.6 35.6 %reshape.81 = f32[2,2,32,2,256,2]{5,4,3,2,1,0:T(8,128)} reshape(f32[4,64,512]{2,1,0:T(8,128)} %fusion.25) | data formatting | bytes 1048576 | tf_op jit(solution)/shard_map/reshape | solution.py:53
  257.2 12.9 %reduce_sum.40 = f32[2,32,256]{2,1,0:T(8,128)} reduce(f32[2,2,32,2,256,2]{5,4,3,2,1,0:T(8,128)} %reshape.81, f32[]{:T(128)} %constant.12.clone.1), dimensions={1,3,5}, to_apply=%region_1.2 | reduce | flops 114688 | bytes 589828 | tf_op jit(solution)/shard_map/reduce_sum | solution.py:53
  272.1 7.2 %collective-permute-start.20 = (f32[1,32,256]{2,1,0:T(8,128)S(1)}, f32[1,32,256]{2,1,0:T(8,128)S(1)}, u32[]{:S(2)}, u32[]{:S(2)}) collective-permute-start(f32[1,32,256]{2,1,0:T(8,128)S(1)} %get-tuple-element.57), channel_id=1, source_target_pairs={{0,8},{8,16},{16,24},{24,32},{32,40},{40,48},{48,56},{56,64},{64,7... | collective-permute-start | bytes 98312 | tf_op jit(solution)/shard_map/ppermute | solution.py:17
  282.1 4.3 collective-permute-start.28
  299.6 4.6 %collective-permute-start.24 = (f32[1,32,256]{2,1,0:T(8,128)S(1)}, f32[1,32,256]{2,1,0:T(8,128)S(1)}, u32[]{:S(2)}, u32[]{:S(2)}) collective-permute-start(f32[1,32,256]{2,1,0:T(8,128)S(1)} %get-tuple-element.55), channel_id=1, source_target_pairs={{0,8},{8,16},{16,24},{24,32},{32,40},{40,48},{48,56},{56,64},{64,7... | collective-permute-start | bytes 98312 | tf_op jit(solution)/shard_map/ppermute | solution.py:17
  304.2 4.6 collective-permute-start.25
  314.2 4.0 collective-permute-start.26
  326.4 4.2 reduce_sum.55
  334.2 4.4 collective-permute-start.32
  338.6 5.5 %collective-permute-start.33 = (f32[1,16,128]{2,1,0:T(8,128)S(1)}, f32[1,16,128]{2,1,0:T(8,128)S(1)}, u32[]{:S(2)}, u32[]{:S(2)}) collective-permute-start(f32[1,16,128]{2,1,0:T(8,128)S(1)} %get-tuple-element.5), channel_id=1, source_target_pairs={{8,0},{16,8},{24,16},{32,24},{40,32},{48,40},{56,48},{64,56},{72,6... | collective-permute-start | bytes 24584 | tf_op jit(solution)/shard_map/ppermute | solution.py:20
  354.3 7.0 %collective-permute-start.36 = (f32[1,16,128]{2,1,0:T(8,128)S(1)}, f32[1,16,128]{2,1,0:T(8,128)S(1)}, u32[]{:S(2)}, u32[]{:S(2)}) collective-permute-start(f32[1,16,128]{2,1,0:T(8,128)S(1)} %fusion.228), channel_id=1, source_target_pairs={{0,8},{8,16},{16,24},{24,32},{32,40},{40,48},{48,56},{56,64},{64,7... | collective-permute-start | bytes 24584 | tf_op jit(solution)/shard_map/ppermute | solution.py:17
  363.8 4.1 collective-permute-done.37
  377.2 3.9 collective-permute-start.40
  383.6 4.1 collective-permute-done.41
  409.4 4.4 collective-permute-done.45
  440.2 5.5 %collective-permute-done.49 = f32[1,64,512]{2,1,0:T(8,128)S(1)} collective-permute-done((f32[1,64,512]{2,1,0:T(8,128)S(1)}, f32[1,64,512]{2,1,0:T(8,128)S(1)}, u32[]{:S(2)}, u32[]{:S(2)}) %collective-permute-start.49) | collective-permute-done | bytes 131104 | tf_op jit(solution)/shard_map/ppermute | solution.py:20
  (213 shorter events, 177.0 us)
Async XLA Ops:
  2.8 110.0 %collective-permute-start = (f32[1,64,512]{2,1,0:T(8,128)}, f32[1,64,512]{2,1,0:T(8,128)S(1)}, u32[]{:S(2)}, u32[]{:S(2)}) collective-permute-start(f32[1,64,512]{2,1,0:T(8,128)} %get-tuple-element.40), channel_id=1, source_target_pairs={{0,8},{8,16},{16,24},{24,32},{32,40},{40,48},{48,56},{56,64},{64,7... | collective-permute-start | bytes 393224 | tf_op jit(solution)/shard_map/ppermute | solution.py:17
  8.8 103.9 %collective-permute-start.2 = (f32[1,64,512]{2,1,0:T(8,128)}, f32[1,64,512]{2,1,0:T(8,128)S(1)}, u32[]{:S(2)}, u32[]{:S(2)}) collective-permute-start(f32[1,64,512]{2,1,0:T(8,128)} %get-tuple-element.39), channel_id=1, source_target_pairs={{8,0},{16,8},{24,16},{32,24},{40,32},{48,40},{56,48},{64,56},{72,6... | collective-permute-start | bytes 393224 | tf_op jit(solution)/shard_map/ppermute | solution.py:20
  10.8 107.3 %collective-permute-start.1 = (f32[1,64,512]{2,1,0:T(8,128)S(1)}, f32[1,64,512]{2,1,0:T(8,128)S(1)}, u32[]{:S(2)}, u32[]{:S(2)}) collective-permute-start(f32[1,64,512]{2,1,0:T(8,128)S(1)} %get-tuple-element.42), channel_id=1, source_target_pairs={{0,8},{8,16},{16,24},{24,32},{32,40},{40,48},{48,56},{56,64},{64,7... | collective-permute-start | bytes 393224 | tf_op jit(solution)/shard_map/ppermute | solution.py:17
  16.0 102.2 %collective-permute-start.3 = (f32[1,64,512]{2,1,0:T(8,128)S(1)}, f32[1,64,512]{2,1,0:T(8,128)S(1)}, u32[]{:S(2)}, u32[]{:S(2)}) collective-permute-start(f32[1,64,512]{2,1,0:T(8,128)S(1)} %get-tuple-element.41), channel_id=1, source_target_pairs={{8,0},{16,8},{24,16},{32,24},{40,32},{48,40},{56,48},{64,56},{72,6... | collective-permute-start | bytes 393224 | tf_op jit(solution)/shard_map/ppermute | solution.py:20
  112.8 12.1 %collective-permute-start.4 = (f32[6,1,512]{2,1,0:T(1,128)S(1)}, f32[6,1,512]{2,1,0:T(1,128)S(1)}, u32[]{:S(2)}, u32[]{:S(2)}) collective-permute-start(f32[6,1,512]{2,1,0:T(1,128)S(1)} %get-tuple-element.28), channel_id=1, source_target_pairs={{0,1},{1,2},{2,3},{3,4},{4,5},{5,6},{6,7},{8,9},{9,10},{10,11},{11... | collective-permute-start | bytes 36872 | tf_op jit(solution)/shard_map/ppermute | solution.py:17
  115.3 9.5 %collective-permute-start.6 = (f32[6,1,512]{2,1,0:T(1,128)S(1)}, f32[6,1,512]{2,1,0:T(1,128)S(1)}, u32[]{:S(2)}, u32[]{:S(2)}) collective-permute-start(f32[6,1,512]{2,1,0:T(1,128)S(1)} %get-tuple-element.27), channel_id=1, source_target_pairs={{1,0},{2,1},{3,2},{4,3},{5,4},{6,5},{7,6},{9,8},{10,9},{11,10},{12... | collective-permute-start | bytes 36872 | tf_op jit(solution)/shard_map/ppermute | solution.py:20
  118.2 7.1 %collective-permute-start.5 = (f32[6,1,512]{2,1,0:T(1,128)S(1)}, f32[6,1,512]{2,1,0:T(1,128)S(1)}, u32[]{:S(2)}, u32[]{:S(2)}) collective-permute-start(f32[6,1,512]{2,1,0:T(1,128)S(1)} %get-tuple-element.29), channel_id=1, source_target_pairs={{0,1},{1,2},{2,3},{3,4},{4,5},{5,6},{6,7},{8,9},{9,10},{10,11},{11... | collective-permute-start | bytes 36872 | tf_op jit(solution)/shard_map/ppermute | solution.py:17
  131.8 10.3 %collective-permute-start.8 = (f32[1,64,512]{2,1,0:T(8,128)S(1)}, f32[1,64,512]{2,1,0:T(8,128)S(1)}, u32[]{:S(2)}, u32[]{:S(2)}) collective-permute-start(f32[1,64,512]{2,1,0:T(8,128)S(1)} %get-tuple-element.37), channel_id=1, source_target_pairs={{0,8},{8,16},{16,24},{24,32},{32,40},{40,48},{48,56},{56,64},{64,7... | collective-permute-start | bytes 393224 | tf_op jit(solution)/shard_map/ppermute | solution.py:17
  139.5 7.8 %collective-permute-start.9 = (f32[1,64,512]{2,1,0:T(8,128)S(1)}, f32[1,64,512]{2,1,0:T(8,128)S(1)}, u32[]{:S(2)}, u32[]{:S(2)}) collective-permute-start(f32[1,64,512]{2,1,0:T(8,128)S(1)} %get-tuple-element.38), channel_id=1, source_target_pairs={{8,0},{16,8},{24,16},{32,24},{40,32},{48,40},{56,48},{64,56},{72,6... | collective-permute-start | bytes 393224 | tf_op jit(solution)/shard_map/ppermute | solution.py:20
  147.3 10.3 %collective-permute-start.10 = (f32[6,1,512]{2,1,0:T(1,128)S(1)}, f32[6,1,512]{2,1,0:T(1,128)S(1)}, u32[]{:S(2)}, u32[]{:S(2)}) collective-permute-start(f32[6,1,512]{2,1,0:T(1,128)S(1)} %get-tuple-element.25), channel_id=1, source_target_pairs={{0,1},{1,2},{2,3},{3,4},{4,5},{5,6},{6,7},{8,9},{9,10},{10,11},{11... | collective-permute-start | bytes 36872 | tf_op jit(solution)/shard_map/ppermute | solution.py:17
  149.3 8.3 %collective-permute-start.11 = (f32[6,1,512]{2,1,0:T(1,128)S(1)}, f32[6,1,512]{2,1,0:T(1,128)S(1)}, u32[]{:S(2)}, u32[]{:S(2)}) collective-permute-start(f32[6,1,512]{2,1,0:T(1,128)S(1)} %get-tuple-element.26), channel_id=1, source_target_pairs={{1,0},{2,1},{3,2},{4,3},{5,4},{6,5},{7,6},{9,8},{10,9},{11,10},{12... | collective-permute-start | bytes 36872 | tf_op jit(solution)/shard_map/ppermute | solution.py:20
  153.3 44.9 %collective-permute-start.16 = (f32[1,32,256]{2,1,0:T(8,128)}, f32[1,32,256]{2,1,0:T(8,128)}, u32[]{:S(2)}, u32[]{:S(2)}) collective-permute-start(f32[1,32,256]{2,1,0:T(8,128)} %get-tuple-element.60), channel_id=1, source_target_pairs={{0,8},{8,16},{16,24},{24,32},{32,40},{40,48},{48,56},{56,64},{64,7... | collective-permute-start | bytes 98312 | tf_op jit(solution)/shard_map/ppermute | solution.py:17
  155.6 42.5 %collective-permute-start.17 = (f32[1,32,256]{2,1,0:T(8,128)}, f32[1,32,256]{2,1,0:T(8,128)}, u32[]{:S(2)}, u32[]{:S(2)}) collective-permute-start(f32[1,32,256]{2,1,0:T(8,128)} %get-tuple-element.59), channel_id=1, source_target_pairs={{8,0},{16,8},{24,16},{32,24},{40,32},{48,40},{56,48},{64,56},{72,6... | collective-permute-start | bytes 98312 | tf_op jit(solution)/shard_map/ppermute | solution.py:20
  160.2 44.4 %collective-permute-start.12 = (f32[1,64,512]{2,1,0:T(8,128)}, f32[1,64,512]{2,1,0:T(8,128)}, u32[]{:S(2)}, u32[]{:S(2)}) collective-permute-start(f32[1,64,512]{2,1,0:T(8,128)} %get-tuple-element.35), channel_id=1, source_target_pairs={{0,8},{8,16},{16,24},{24,32},{32,40},{40,48},{48,56},{56,64},{64,7... | collective-permute-start | bytes 393224 | tf_op jit(solution)/shard_map/ppermute | solution.py:17
  165.2 39.4 %collective-permute-start.13 = (f32[1,64,512]{2,1,0:T(8,128)}, f32[1,64,512]{2,1,0:T(8,128)}, u32[]{:S(2)}, u32[]{:S(2)}) collective-permute-start(f32[1,64,512]{2,1,0:T(8,128)} %get-tuple-element.36), channel_id=1, source_target_pairs={{8,0},{16,8},{24,16},{32,24},{40,32},{48,40},{56,48},{64,56},{72,6... | collective-permute-start | bytes 393224 | tf_op jit(solution)/shard_map/ppermute | solution.py:20
  198.9 13.9 %collective-permute-start.18 = (f32[4,1,256]{2,1,0:T(1,128)S(1)}, f32[4,1,256]{2,1,0:T(1,128)S(1)}, u32[]{:S(2)}, u32[]{:S(2)}) collective-permute-start(f32[4,1,256]{2,1,0:T(1,128)S(1)} %get-tuple-element.50), channel_id=1, source_target_pairs={{0,1},{1,2},{2,3},{3,4},{4,5},{5,6},{6,7},{8,9},{9,10},{10,11},{11... | collective-permute-start | bytes 12296 | tf_op jit(solution)/shard_map/ppermute | solution.py:17
  202.6 10.2 %collective-permute-start.19 = (f32[4,1,256]{2,1,0:T(1,128)S(1)}, f32[4,1,256]{2,1,0:T(1,128)S(1)}, u32[]{:S(2)}, u32[]{:S(2)}) collective-permute-start(f32[4,1,256]{2,1,0:T(1,128)S(1)} %get-tuple-element.49), channel_id=1, source_target_pairs={{1,0},{2,1},{3,2},{4,3},{5,4},{6,5},{7,6},{9,8},{10,9},{11,10},{12... | collective-permute-start | bytes 12296 | tf_op jit(solution)/shard_map/ppermute | solution.py:20
  205.4 9.1 %collective-permute-start.14 = (f32[6,1,512]{2,1,0:T(1,128)S(1)}, f32[6,1,512]{2,1,0:T(1,128)S(1)}, u32[]{:S(2)}, u32[]{:S(2)}) collective-permute-start(f32[6,1,512]{2,1,0:T(1,128)S(1)} %get-tuple-element.23), channel_id=1, source_target_pairs={{0,1},{1,2},{2,3},{3,4},{4,5},{5,6},{6,7},{8,9},{9,10},{10,11},{11... | collective-permute-start | bytes 36872 | tf_op jit(solution)/shard_map/ppermute | solution.py:17
  272.1 18.0 %collective-permute-start.20 = (f32[1,32,256]{2,1,0:T(8,128)S(1)}, f32[1,32,256]{2,1,0:T(8,128)S(1)}, u32[]{:S(2)}, u32[]{:S(2)}) collective-permute-start(f32[1,32,256]{2,1,0:T(8,128)S(1)} %get-tuple-element.57), channel_id=1, source_target_pairs={{0,8},{8,16},{16,24},{24,32},{32,40},{40,48},{48,56},{56,64},{64,7... | collective-permute-start | bytes 98312 | tf_op jit(solution)/shard_map/ppermute | solution.py:17
  279.3 10.8 %collective-permute-start.21 = (f32[1,32,256]{2,1,0:T(8,128)S(1)}, f32[1,32,256]{2,1,0:T(8,128)S(1)}, u32[]{:S(2)}, u32[]{:S(2)}) collective-permute-start(f32[1,32,256]{2,1,0:T(8,128)S(1)} %get-tuple-element.58), channel_id=1, source_target_pairs={{8,0},{16,8},{24,16},{32,24},{40,32},{48,40},{56,48},{64,56},{72,6... | collective-permute-start | bytes 98312 | tf_op jit(solution)/shard_map/ppermute | solution.py:20
  282.1 26.7 %collective-permute-start.28 = (f32[1,16,128]{2,1,0:T(8,128)S(1)}, f32[1,16,128]{2,1,0:T(8,128)S(1)}, u32[]{:S(2)}, u32[]{:S(2)}) collective-permute-start(f32[1,16,128]{2,1,0:T(8,128)S(1)} %bitcast_multiply_fusion), channel_id=1, source_target_pairs={{0,8},{8,16},{16,24},{24,32},{32,40},{40,48},{48,56},{56,64},{64,7... | collective-permute-start | bytes 24584 | tf_op jit(solution)/shard_map/ppermute | solution.py:17
  286.4 22.4 %collective-permute-start.29 = (f32[1,16,128]{2,1,0:T(8,128)S(1)}, f32[1,16,128]{2,1,0:T(8,128)S(1)}, u32[]{:S(2)}, u32[]{:S(2)}) collective-permute-start(f32[1,16,128]{2,1,0:T(8,128)S(1)} %bitcast_multiply_fusion), channel_id=1, source_target_pairs={{8,0},{16,8},{24,16},{32,24},{40,32},{48,40},{56,48},{64,56},{72,6... | collective-permute-start | bytes 24584 | tf_op jit(solution)/shard_map/ppermute | solution.py:20
  299.6 14.5 %collective-permute-start.24 = (f32[1,32,256]{2,1,0:T(8,128)S(1)}, f32[1,32,256]{2,1,0:T(8,128)S(1)}, u32[]{:S(2)}, u32[]{:S(2)}) collective-permute-start(f32[1,32,256]{2,1,0:T(8,128)S(1)} %get-tuple-element.55), channel_id=1, source_target_pairs={{0,8},{8,16},{16,24},{24,32},{32,40},{40,48},{48,56},{56,64},{64,7... | collective-permute-start | bytes 98312 | tf_op jit(solution)/shard_map/ppermute | solution.py:17
  304.2 9.9 %collective-permute-start.25 = (f32[1,32,256]{2,1,0:T(8,128)S(1)}, f32[1,32,256]{2,1,0:T(8,128)S(1)}, u32[]{:S(2)}, u32[]{:S(2)}) collective-permute-start(f32[1,32,256]{2,1,0:T(8,128)S(1)} %get-tuple-element.56), channel_id=1, source_target_pairs={{8,0},{16,8},{24,16},{32,24},{40,32},{48,40},{56,48},{64,56},{72,6... | collective-permute-start | bytes 98312 | tf_op jit(solution)/shard_map/ppermute | solution.py:20
  308.8 11.3 %collective-permute-start.30 = (f32[3,1,128]{2,1,0:T(1,128)S(1)}, f32[3,1,128]{2,1,0:T(1,128)S(1)}, u32[]{:S(2)}, u32[]{:S(2)}) collective-permute-start(f32[3,1,128]{2,1,0:T(1,128)S(1)} %get-tuple-element.68), channel_id=1, source_target_pairs={{0,1},{1,2},{2,3},{3,4},{4,5},{5,6},{6,7},{8,9},{9,10},{10,11},{11... | collective-permute-start | bytes 4616 | tf_op jit(solution)/shard_map/ppermute | solution.py:17
  310.8 9.4 %collective-permute-start.31 = (f32[3,1,128]{2,1,0:T(1,128)S(1)}, f32[3,1,128]{2,1,0:T(1,128)S(1)}, u32[]{:S(2)}, u32[]{:S(2)}) collective-permute-start(f32[3,1,128]{2,1,0:T(1,128)S(1)} %get-tuple-element.67), channel_id=1, source_target_pairs={{1,0},{2,1},{3,2},{4,3},{5,4},{6,5},{7,6},{9,8},{10,9},{11,10},{12... | collective-permute-start | bytes 4616 | tf_op jit(solution)/shard_map/ppermute | solution.py:20
  314.2 6.7 %collective-permute-start.26 = (f32[4,1,256]{2,1,0:T(1,128)S(1)}, f32[4,1,256]{2,1,0:T(1,128)S(1)}, u32[]{:S(2)}, u32[]{:S(2)}) collective-permute-start(f32[4,1,256]{2,1,0:T(1,128)S(1)} %get-tuple-element.45), channel_id=1, source_target_pairs={{0,1},{1,2},{2,3},{3,4},{4,5},{5,6},{6,7},{8,9},{9,10},{10,11},{11... | collective-permute-start | bytes 12296 | tf_op jit(solution)/shard_map/ppermute | solution.py:17
  334.2 9.9 %collective-permute-start.32 = (f32[1,16,128]{2,1,0:T(8,128)S(1)}, f32[1,16,128]{2,1,0:T(8,128)S(1)}, u32[]{:S(2)}, u32[]{:S(2)}) collective-permute-start(f32[1,16,128]{2,1,0:T(8,128)S(1)} %get-tuple-element.5), channel_id=1, source_target_pairs={{0,8},{8,16},{16,24},{24,32},{32,40},{40,48},{48,56},{56,64},{64,7... | collective-permute-start | bytes 24584 | tf_op jit(solution)/shard_map/ppermute | solution.py:17
  354.3 9.5 %collective-permute-start.36 = (f32[1,16,128]{2,1,0:T(8,128)S(1)}, f32[1,16,128]{2,1,0:T(8,128)S(1)}, u32[]{:S(2)}, u32[]{:S(2)}) collective-permute-start(f32[1,16,128]{2,1,0:T(8,128)S(1)} %fusion.228), channel_id=1, source_target_pairs={{0,8},{8,16},{16,24},{24,32},{32,40},{40,48},{48,56},{56,64},{64,7... | collective-permute-start | bytes 24584 | tf_op jit(solution)/shard_map/ppermute | solution.py:17
  361.3 6.6 %collective-permute-start.37 = (f32[1,16,128]{2,1,0:T(8,128)S(1)}, f32[1,16,128]{2,1,0:T(8,128)S(1)}, u32[]{:S(2)}, u32[]{:S(2)}) collective-permute-start(f32[1,16,128]{2,1,0:T(8,128)S(1)} %fusion.228), channel_id=1, source_target_pairs={{8,0},{16,8},{24,16},{32,24},{40,32},{48,40},{56,48},{64,56},{72,6... | collective-permute-start | bytes 24584 | tf_op jit(solution)/shard_map/ppermute | solution.py:20
  406.9 6.9 %collective-permute-start.45 = (f32[1,32,256]{2,1,0:T(8,128)S(1)}, f32[1,32,256]{2,1,0:T(8,128)S(1)}, u32[]{:S(2)}, u32[]{:S(2)}) collective-permute-start(f32[1,32,256]{2,1,0:T(8,128)S(1)} %get-tuple-element.52), channel_id=1, source_target_pairs={{8,0},{16,8},{24,16},{32,24},{40,32},{48,40},{56,48},{64,56},{72,6... | collective-permute-start | bytes 98312 | tf_op jit(solution)/shard_map/ppermute | solution.py:20
  437.5 8.2 %collective-permute-start.49 = (f32[1,64,512]{2,1,0:T(8,128)S(1)}, f32[1,64,512]{2,1,0:T(8,128)S(1)}, u32[]{:S(2)}, u32[]{:S(2)}) collective-permute-start(f32[1,64,512]{2,1,0:T(8,128)S(1)} %get-tuple-element.32), channel_id=1, source_target_pairs={{8,0},{16,8},{24,16},{32,24},{40,32},{48,40},{56,48},{64,56},{72,6... | collective-permute-start | bytes 393224 | tf_op jit(solution)/shard_map/ppermute | solution.py:20
  (46 other events, 652.6 us)
where the time goes:
time: 462 us; the launch traced here: 457 us
  starting transfers between devices  175 us (38%)
  local copies, waits for them, and re-layouts  147 us (32%)
  other arithmetic  80.9 us (18%)
  waiting for transfers between devices  53.1 us (11%)
    ppermute x26, starting transfers between devices, extended(): lax.ppermute(lax.slice_in_dim(block, block.shape[dim] - width, None, axis...  101 us
    ppermute x26, starting transfers between devices, extended(): lax.ppermute(lax.slice_in_dim(block, 0, width, axis=dim), axis, backward)  74.1 us
    reshape x2, local copies, waits for them, and re-layouts, coarsen_sum(): values.reshape(size_x // 2, 2, size_z // 2, 2, size_y // 2, 2)  70.5 us
    ppermute x26, waiting for transfers between devices, extended(): lax.ppermute(lax.slice_in_dim(block, 0, width, axis=dim), axis, backward)  53 us
    reshape x1, local copies, waits for them, and re-layouts, coarsen_max(): values.reshape(size_x // 2, 2, size_z // 2, 2, size_y // 2, 2)  34.8 us
    reduce_sum x6, other arithmetic, coarsen_sum(): values.reshape(size_x // 2, 2, size_z // 2, 2, size_y // 2, 2)  32.9 us
    reduce_max x4, other arithmetic, coarsen_max(): values.reshape(size_x // 2, 2, size_z // 2, 2, size_y // 2, 2)  22 us
    reduce_max x2, local copies, waits for them, and re-layouts, coarsen_max(): values.reshape(size_x // 2, 2, size_z // 2, 2, size_y // 2, 2)  14.7 us
  transfers between devices with their start and end apart: 52, of which 15 were waited for; matrix products, arithmetic and copies ran while one was open for 30% of the time, Pallas kernels for 0%

commit v1 on v0

v1 whole, which is shorter than its diff:
```python
import functools

import jax
import jax.numpy as jnp
from jax import lax
from jax.experimental import pallas as pl
from jax.experimental.pallas import tpu as pltpu
from jax.sharding import PartitionSpec as P

FLOOR_SUM = 0.1
LANES = 128
F32 = jnp.float32
MESH = pl.DeviceIdType.MESH

FINE_X, FINE_Z = 1, 8
MID_X, MID_Z = 2, 16
COARSE_X, COARSE_Z = 4, 16
REACH = 4


def y_next(values):
    rolled = pltpu.roll(values, LANES - 1, 2)
    if values.shape[0] == 1:
        return rolled
    lane = lax.broadcasted_iota(jnp.int32, values.shape, 2)
    return jnp.where(lane == LANES - 1, jnp.concatenate([rolled[1:], rolled[:1]], 0), rolled)


def y_prev(values):
    rolled = pltpu.roll(values, 1, 2)
    if values.shape[0] == 1:
        return rolled
    lane = lax.broadcasted_iota(jnp.int32, values.shape, 2)
    return jnp.where(lane == 0, jnp.concatenate([rolled[-1:], rolled[:-1]], 0), rolled)


def conduct(left, right, spacing):
    return (2.0 * spacing) * left * right / jnp.maximum(left + right, FLOOR_SUM)


class Level:
    def __init__(self, spacing, perm, tx, tz, ty, diag, inv):
        self.spacing, self.storage = spacing, 0.5 * spacing**3
        self.perm, self.tx, self.tz, self.ty = perm, tx, tz, ty
        self.diag, self.inv = diag, inv

    def make_tx(self, plane, row, rows):
        at = pl.ds(row, rows)
        self.tx[plane, :, at, :] = conduct(
            self.perm[plane - 1, :, at, :], self.perm[plane, :, at, :], self.spacing
        )

    def make_tz(self, plane, row, rows):
        self.tz[plane, :, pl.ds(row, rows), :] = conduct(
            self.perm[plane, :, pl.ds(row - 1, rows), :],
            self.perm[plane, :, pl.ds(row, rows), :],
            self.spacing,
        )

    def make_ty(self, plane, row, rows):
        here = self.perm[plane, :, pl.ds(row, rows), :]
        lane = lax.broadcasted_iota(jnp.int32, here.shape, 2)
        block = lax.broadcasted_iota(jnp.int32, here.shape, 0)
        last = (lane == LANES - 1) & (block == here.shape[0] - 1)
        value = conduct(here, y_next(here), self.spacing)
        self.ty[plane, :, pl.ds(row, rows), :] = jnp.where(last, 0.0, value)

    def make_diag(self, plane, row, rows):
        at, after = pl.ds(row, rows), pl.ds(row + 1, rows)
        along = self.ty[plane, :, at, :]
        total = self.storage + self.tx[plane, :, at, :] + self.tx[plane + 1, :, at, :]
        total = total + self.tz[plane, :, at, :] + self.tz[plane, :, after, :]
        total = total + along + y_prev(along)
        if self.diag is not None:
            self.diag[plane, :, at, :] = total
        self.inv[plane, :, at, :] = jnp.where(self.perm[plane, :, at, :] > 0.0, 0.8 / total, 0.0)

    def flow(self, field, plane, row, rows):
        at, after = pl.ds(row, rows), pl.ds(row + 1, rows)
        here = field[plane, :, at, :]
        along = self.ty[plane, :, at, :]
        total = self.tx[plane, :, at, :] * field[plane - 1, :, at, :]
        total = total + self.tx[plane + 1, :, at, :] * field[plane + 1, :, at, :]
        total = total + self.tz[plane, :, at, :] * field[plane, :, pl.ds(row - 1, rows), :]
        total = total + self.tz[plane, :, after, :] * field[plane, :, after, :]
        total = total + along * y_next(here) + y_prev(along * here)
        return here, total


def take(values, index):
    return jnp.take_along_axis(values, index, axis=1, mode="promise_in_bounds")


def coarsen(ref, plane, block, row, rows):
    lane = lax.broadcasted_iota(jnp.int32, (rows, LANES), 1)
    index = lax.rem(2 * lane, LANES)
    parts = []
    for half in (0, 1):
        total = None
        for step_x in (0, 1):
            for step_z in (0, 1):
                piece = ref[plane + step_x, 2 * block + half, pl.ds(row + step_z, rows, stride=2), :]
                total = piece if total is None else total + piece
        parts.append(take(total + pltpu.roll(total, LANES - 1, 1), index))
    return jnp.where(lane < LANES // 2, parts[0], parts[1])


def refine_rows(target, target_plane, target_block, values):
    rows = values.shape[0]
    lane = lax.broadcasted_iota(jnp.int32, values.shape, 1)
    spread = take(values, (LANES // 2) * (target_block % 2) + lane // 2)
    target[target_plane, target_block, pl.ds(0, rows, stride=2), :] = spread
    target[target_plane, target_block, pl.ds(1, rows, stride=2), :] = spread


def kernel(
    n_wide, n_narrow,
    pressure, source, permeability, active_mask, out,
    raw, act, rhs, v0, v1, v2, v3, perm, tx, tz, ty, diag, inv, resid,
    zs1, zr1, zs2, zr2, zs3, zr3,
    m_raw, m_perm, m_tx, m_tz, m_ty, m_diag, m_inv, m_rhs, m_f1, m_f2, m_u, m_fin, m_refx, m_refz, m_res, rc, rf,
    c_perm, c_tx, c_tz, c_ty, c_inv, c_f1, c_f2, c_f3, c_f4,
    load_sem, send_sem, recv_sem,
):
    wide, narrow = lax.axis_index("wide"), lax.axis_index("narrow")
    fine = Level(1.0, perm, tx, tz, ty, diag, inv)
    mid = Level(2.0, m_perm, m_tx, m_tz, m_ty, m_diag, m_inv)
    coarse = Level(4.0, c_perm, c_tx, c_tz, c_ty, None, c_inv)
    slots = [0]

    def exists(dx, dz):
        ok = None
        for step, here, count in ((dx, wide, n_wide), (dz, narrow, n_narrow)):
            if step == 0:
                continue
            one = here + step < count if step > 0 else here + step >= 0
            ok = one if ok is None else ok & one
        return ok

    class Swap:
        def __init__(self, dx, dz, src, dst):
            slot = slots[0]
            slots[0] += 1
            self.ok, self.back = exists(dx, dz), exists(-dx, -dz)
            self.copy = pltpu.make_async_remote_copy(
                src_ref=src, dst_ref=dst, send_sem=send_sem.at[slot], recv_sem=recv_sem.at[slot],
                device_id=(wide + dx, narrow + dz), device_id_type=MESH,
            )

        def start(self):
            pl.when(self.ok)(self.copy.start)

        def wait_recv(self):
            pl.when(self.back)(self.copy.wait_recv)

        def wait_send(self):
            pl.when(self.ok)(self.copy.wait_send)

    everyone = []

    def swaps(items):
        made = [Swap(*item) for item in items]
        everyone.extend(made)
        return made

    def start(group):
        for one in group:
            one.start()

    def wait(group):
        for one in group:
            one.wait_recv()

    peers = [(dx, dz) for dx in range(-REACH, REACH + 1) for dz in (-1, 0, 1) if (dx, dz) != (0, 0)]

    loads = []
    for which, (src, dst) in enumerate(
        ((permeability, raw), (active_mask, act), (pressure, v0), (source, rhs))
    ):
        for block in range(4):
            into = dst.at[pl.ds(1, 4), block, pl.ds(8, 64), :] if dst is v0 else dst.at[:, block, :, :]
            copy = pltpu.make_async_copy(
                src.at[:, :, pl.ds(block * LANES, LANES)], into, load_sem.at[which * 4 + block]
            )
            copy.start()
            loads.append(copy)

    for ref in (m_perm, m_f1, m_refx, m_refz, c_perm, c_f1, zr1, zr2, zr3):
        ref[...] = jnp.zeros(ref.shape, F32)
    for ref in (m_u, m_f2, c_f2, c_f3):
        ref[...] = jnp.zeros(ref.shape, F32)

    barrier = pltpu.get_barrier_semaphore()
    for dx, dz in peers:
        @pl.when(exists(dx, dz))
        def _():
            pl.semaphore_signal(barrier, inc=1, device_id=(wide + dx, narrow + dz), device_id_type=MESH)

    low_edge, high_edge = wide == 0, wide == n_wide - 1
    for plane, edge in ((0, low_edge), (5, high_edge)):
        @pl.when(edge)
        def _():
            for ref in (perm, v0, v1, v2):
                ref[plane] = jnp.zeros(ref.shape[1:], F32)

    def chunks(first, last, body):
        def step(k, carry):
            body(pl.multiple_of(k * 8, 8))
            return carry
        lax.fori_loop(first // 8, last // 8, step, 0)

    for copy in loads[:8]:
        copy.wait()

    def mask_perm(row):
        for plane in range(4):
            value = raw[plane, :, pl.ds(row, 8), :] * act[plane, :, pl.ds(row, 8), :].astype(F32)
            perm[plane + 1, :, pl.ds(row + 8, 8), :] = value

    chunks(0, 64, mask_perm)
    for copy in loads[8:12]:
        copy.wait()

    def pack(target, field):
        for side, row in ((0, 8), (1, 71)):
            for plane in range(4):
                for block in range(4):
                    target[side, pl.ds(plane * 4 + block, 1), :] = field[plane + 1, block, pl.ds(row, 1), :]

    def unpack(field, buffer):
        for side, row in ((0, 7), (1, 72)):
            for plane in range(4):
                for block in range(4):
                    field[plane + 1, block, pl.ds(row, 1), :] = buffer[side, pl.ds(plane * 4 + block, 1), :]

    def fine_x(field):
        rows = pl.ds(8, 64)
        return swaps([
            (-1, 0, field.at[1, :, rows, :], field.at[5, :, rows, :]),
            (1, 0, field.at[4, :, rows, :], field.at[0, :, rows, :]),
        ])

    def fine_z(send, recv):
        return swaps([(0, -1, send.at[0], recv.at[1]), (0, 1, send.at[1], recv.at[0])])

    pack(zs1.at[0], perm)
    pack(zs1.at[1], v0)

    count_x = jnp.minimum(wide, REACH) + jnp.minimum(n_wide - 1 - wide, REACH) + 1
    count_z = jnp.minimum(narrow, 1) + jnp.minimum(n_narrow - 1 - narrow, 1) + 1
    pl.semaphore_wait(barrier, count_x * count_z - 1)

    perm_x, v0_x = fine_x(perm), fine_x(v0)
    perm_z = fine_z(zs1.at[0], zr1.at[0])
    v0_z = fine_z(zs1.at[1], zr1.at[1])
    start(perm_x + v0_x + perm_z + v0_z)

    for plane in range(2):
        for block in range(2):
            value = coarsen(raw, 2 * plane, block, 0, 32) * 0.125
            m_raw[plane, block] = value
            some = coarsen(perm, 2 * plane + 1, block, 8, 32) > 0.0
            m_perm[plane + 2, block, pl.ds(16, 32), :] = jnp.where(some, value, 0.0)

    def mid_swaps(ref):
        own, low, high = pl.ds(16, 32), pl.ds(16, 8), pl.ds(40, 8)
        below, above = pl.ds(8, 8), pl.ds(48, 8)
        two = pl.ds(2, 2)
        return swaps([
            (-1, 0, ref.at[two, :, own, :], ref.at[pl.ds(4, 2), :, own, :]),
            (1, 0, ref.at[two, :, own, :], ref.at[pl.ds(0, 2), :, own, :]),
            (0, -1, ref.at[two, :, low, :], ref.at[two, :, above, :]),
            (0, 1, ref.at[two, :, high, :], ref.at[two, :, below, :]),
            (-1, -1, ref.at[2, :, low, :], ref.at[4, :, above, :]),
            (-1, 1, ref.at[2, :, high, :], ref.at[4, :, below, :]),
            (1, -1, ref.at[3, :, low, :], ref.at[1, :, above, :]),
            (1, 1, ref.at[3, :, high, :], ref.at[1, :, below, :]),
        ])

    def coarse_swaps(ref):
        mine = {0: pl.ds(16, 16), -1: pl.ds(16, 8), 1: pl.ds(24, 8)}
        theirs = {0: pl.ds(16, 16), -1: pl.ds(32, 8), 1: pl.ds(8, 8)}
        return swaps([
            (dx, dz, ref.at[4, :, mine[dz], :], ref.at[4 - dx, :, theirs[dz], :])
            for dx, dz in sorted(peers, key=lambda one: -abs(one[0]))
        ])

    mid_perm_swaps = mid_swaps(m_perm)
    start(mid_perm_swaps)
    some = coarsen(m_perm, 2, 0, 16, 16) > 0.0
    value = coarsen(m_raw, 0, 0, 0, 16) * 0.125
    c_perm[4, 0, pl.ds(16, 16), :] = jnp.where(some, value, 0.0)
    coarse_perm_swaps = coarse_swaps(c_perm)
    start(coarse_perm_swaps)

    def inner(row):
        for plane in range(1, 5):
            fine.make_ty(plane, row, 8)
            if plane > 1:
                fine.make_tx(plane, row, 8)

    chunks(8, 72, inner)

    def inner_z(row):
        for plane in range(1, 5):
            fine.make_tz(plane, row, 8)

    chunks(16, 72, inner_z)

    wait(perm_z + v0_z)
    unpack(perm, zr1.at[0])
    unpack(v0, zr1.at[1])
    inner_z(8)
    inner_z(72)
    for copy in loads[12:]:
        copy.wait()
    chunks(8, 72, lambda row: [fine.make_diag(plane, row, 8) for plane in (2, 3)])

    def relax(old, new, planes, first):
        def body(row):
            at = pl.ds(row, 8)
            for plane in planes:
                here, total = fine.flow(old, plane, row, 8)
                if first:
                    here = jnp.where(perm[plane, :, at, :] > 0.0, here, 0.0)
                force = rhs[plane - 1, :, pl.ds(row - 8, 8), :] + total
                new[plane, :, at, :] = 0.2 * here + inv[plane, :, at, :] * force
        chunks(8, 72, body)

    wait(perm_x)

    def outer(row):
        fine.make_tx(1, row, 8)
        fine.make_tx(5, row, 8)
        fine.make_diag(1, row, 8)
        fine.make_diag(4, row, 8)

    chunks(8, 72, outer)
    wait(v0_x)

    def sweep(old, new, first, send, recv):
        relax(old, new, (1, 4), first)
        by_x = fine_x(new)
        start(by_x)
        relax(old, new, (2, 3), first)
        pack(send, new)
        by_z = fine_z(send, recv)
        start(by_z)
        return by_x, by_z

    v1_x, v1_z = sweep(v0, v1, True, zs2, zr2)

    wait(mid_perm_swaps)
    for plane in range(1, 6):
        mid.make_tx(plane, 8, 48)
    for plane in range(1, 5):
        mid.make_ty(plane, 8, 48)
        mid.make_tz(plane, 8, 56)
        mid.make_diag(plane, 8, 48)

    wait(v1_z)
    unpack(v1, zr2)
    wait(v1_x)
    v2_x, v2_z = sweep(v1, v2, False, zs3, zr3)

    wait(coarse_perm_swaps)
    for plane in range(1, 9):
        coarse.make_tx(plane, 8, 32)
    for plane in range(1, 8):
        coarse.make_ty(plane, 8, 32)
        coarse.make_tz(plane, 8, 40)
        coarse.make_diag(plane, 8, 32)

    def residual(planes):
        def body(row):
            at = pl.ds(row, 8)
            for plane in planes:
                here, total = fine.flow(v2, plane, row, 8)
                value = rhs[plane - 1, :, pl.ds(row - 8, 8), :] + total - diag[plane, :, at, :] * here
                resid[plane - 1, :, pl.ds(row - 8, 8), :] = jnp.where(perm[plane, :, at, :] > 0.0, value, 0.0)
        chunks(8, 72, body)

    wait(v2_z)
    unpack(v2, zr3)
    residual((2, 3))
    wait(v2_x)
    residual((1, 4))

    own = pl.ds(16, 32)
    for plane in range(2):
        for block in range(2):
            value = coarsen(resid, 2 * plane, block, 0, 32)
            value = jnp.where(m_perm[plane + 2, block, own, :] > 0.0, value, 0.0)
            m_rhs[plane, block] = value
            m_f1[plane + 2, block, own, :] = m_inv[plane + 2, block, own, :] * value
    mid_f1_swaps = mid_swaps(m_f1)
    start(mid_f1_swaps)
    wait(mid_f1_swaps)
    for plane in range(1, 5):
        here, total = mid.flow(m_f1, plane, 8, 48)
        m_f2[plane, :, pl.ds(8, 48), :] = 1.2 * here + m_inv[plane, :, pl.ds(8, 48), :] * total
    for plane in range(2):
        here, total = mid.flow(m_f2, plane + 2, 16, 32)
        value = m_rhs[plane] + total - m_diag[plane + 2, :, own, :] * here
        m_res[plane] = jnp.where(m_perm[plane + 2, :, own, :] > 0.0, value, 0.0)

    here = pl.ds(16, 16)
    value = coarsen(m_res, 0, 0, 0, 16)
    c_f1[4, 0, here, :] = c_inv[4, 0, here, :] * value
    coarse_f1_swaps = coarse_swaps(c_f1)
    start(coarse_f1_swaps)
    tall = pl.ds(8, 48)
    two = pl.ds(2, 2)
    mid_f2_swaps = swaps([
        (-1, 0, m_f2.at[two, :, tall, :], m_refx.at[1]),
        (1, 0, m_f2.at[two, :, tall, :], m_refx.at[0]),
        (0, -1, m_f2.at[two, :, pl.ds(16, 8), :], m_refz.at[1]),
        (0, 1, m_f2.at[two, :, pl.ds(40, 8), :], m_refz.at[0]),
    ])
    start(mid_f2_swaps)
    wait(coarse_f1_swaps)
    body = pl.ds(8, 32)
    for old, new, first, last in ((c_f1, c_f2, 1, 7), (c_f2, c_f3, 2, 6), (c_f3, c_f4, 3, 5)):
        for plane in range(first, last + 1):
            value, total = coarse.flow(old, plane, 8, 32)
            value = 1.2 * value if old is c_f1 else 0.2 * value + c_f1[plane, :, body, :]
            new[plane, :, body, :] = value + c_inv[plane, :, body, :] * total

    for plane in range(3):
        for block in range(2):
            refine_rows(rc, plane, block, c_f4[plane + 3, 0, body, :])
    wait(mid_f2_swaps)
    for plane in range(6):
        for block in range(2):
            add = jnp.where(m_perm[plane, block, tall, :] > 0.0, rc[plane // 2, block, tall, :], 0.0)
            if plane in (2, 3):
                base = jnp.concatenate([
                    m_refz[0, plane - 2, block], m_f2[plane, block, own, :], m_refz[1, plane - 2, block]
                ], 0)
            else:
                base = m_refx[plane // 4, plane % 2, block]
            m_u[plane, block, tall, :] = base + add
    for plane in range(1, 5):
        value, total = mid.flow(m_u, plane, 8, 48)
        value = 0.2 * value + m_f1[plane, :, tall, :] + m_inv[plane, :, tall, :] * total
        m_fin[plane, :, tall, :] = value

    for plane in range(4):
        for block in range(4):
            refine_rows(rf, plane, block, m_fin[plane + 1, block // 2, pl.ds(12, 40), :])

    def correct(row):
        at = pl.ds(row, 8)
        for plane in range(6):
            add = jnp.where(perm[plane, :, at, :] > 0.0, rf[(plane + 1) // 2, :, at, :], 0.0)
            v3[plane, :, at, :] = v2[plane, :, at, :] + add

    chunks(0, 80, correct)

    def finish(row):
        at = pl.ds(row, 8)
        for plane in range(1, 5):
            value, total = fine.flow(v3, plane, row, 8)
            force = rhs[plane - 1, :, pl.ds(row - 8, 8), :] + total
            value = 0.2 * value + inv[plane, :, at, :] * force
            for block in range(4):
                out[plane - 1, pl.ds(pl.multiple_of(row - 8, 8), 8), pl.ds(block * LANES, LANES)] = value[block]

    chunks(8, 72, finish)
    for one in everyone:
        one.wait_send()


def per_device(n_wide, n_narrow, pressure, source, permeability, active_mask):
    def vmem(*shape, dtype=F32):
        return pltpu.VMEM(shape, dtype)

    fine_pad, fine_own = (6, 4, 80, LANES), (4, 4, 64, LANES)
    mid_pad, mid_own = (6, 2, 64, LANES), (2, 2, 32, LANES)
    coarse_pad = (9, 1, 48, LANES)
    scratch = [vmem(*fine_own), vmem(*fine_own, dtype=jnp.int32), vmem(*fine_own)]
    scratch += [vmem(*fine_pad) for _ in range(10)] + [vmem(*fine_own)]
    scratch += [vmem(2, 2, 16, LANES), vmem(2, 2, 16, LANES)] + [vmem(2, 16, LANES) for _ in range(4)]
    scratch += [vmem(*mid_own)] + [vmem(*mid_pad) for _ in range(6)] + [vmem(*mid_own)]
    scratch += [vmem(*mid_pad) for _ in range(4)]
    scratch += [vmem(2, 2, 2, 48, LANES), vmem(2, 2, 2, 8, LANES), vmem(*mid_own)]
    scratch += [vmem(3, 2, 64, LANES), vmem(4, 4, 80, LANES)]
    scratch += [vmem(*coarse_pad) for _ in range(9)]
    scratch += [pltpu.SemaphoreType.DMA((16,)), pltpu.SemaphoreType.DMA((96,)), pltpu.SemaphoreType.DMA((96,))]
    return pl.pallas_call(
        functools.partial(kernel, n_wide, n_narrow),
        out_shape=jax.ShapeDtypeStruct(pressure.shape, F32),
        in_specs=[pl.BlockSpec(memory_space=pl.ANY)] * 4,
        out_specs=pl.BlockSpec(memory_space=pltpu.VMEM),
        scratch_shapes=scratch,
        compiler_params=pltpu.CompilerParams(
            collective_id=0, has_side_effects=True, vmem_limit_bytes=48 * 1024 * 1024
        ),
        name="vcycle",
    )(pressure, source, permeability, active_mask)


def solution(mesh):
    spec = P("wide", "narrow", None)
    return jax.shard_map(
        functools.partial(per_device, mesh.shape["wide"], mesh.shape["narrow"]),
        mesh=mesh, in_specs=(spec,) * 4, out_specs=spec, check_vma=False,
    )
```

time: 462 us -> 46.7 us (0.10); the launches traced: 457 us -> 46.4 us
  starting transfers between devices: 175 us -> 0 us
  local copies, waits for them, and re-layouts: 147 us -> 4.96 us
  other arithmetic: 80.9 us -> 0 us
  waiting for transfers between devices: 53.1 us -> 0 us
  Pallas kernels: 0 us -> 41.4 us
    ppermute x52 -> x0, starting transfers between devices: 175 us -> none  [the longest x26 101 us: extended(): lax.ppermute(lax.slice_in_dim(block, block.shape[dim] - width, None, axis...]
    reshape x6 -> x0, local copies, waits for them, and re-layouts: 111 us -> none  [the longest x2 70.5 us: coarsen_sum(): values.reshape(size_x // 2, 2, size_z // 2, 2, size_y // 2, 2)]
    ppermute x52 -> x0, waiting for transfers between devices: 53.1 us -> none  [the longest x26 53 us: extended(): lax.ppermute(lax.slice_in_dim(block, 0, width, axis=dim), axis, backward)]
    pallas_call x0 -> x1, Pallas kernels: none -> 41.4 us  [per_device(): pl.pallas_call(functools.partial(kernel, n_wide, n_narrow), out_shape=jax...]
    reduce_sum x6 -> x0, other arithmetic: 32.9 us -> none  [coarsen_sum(): values.reshape(size_x // 2, 2, size_z // 2, 2, size_y // 2, 2)]
    reduce_max x4 -> x0, other arithmetic: 22 us -> none  [coarsen_max(): values.reshape(size_x // 2, 2, size_z // 2, 2, size_y // 2, 2)]
    reduce_max x2 -> x0, local copies, waits for them, and re-layouts: 14.7 us -> none  [coarsen_max(): values.reshape(size_x // 2, 2, size_z // 2, 2, size_y // 2, 2)]
    mul x12 -> x0, other arithmetic: 14.6 us -> none  [the longest x10 11.9 us: relax_cells(): active * (centre_field + RELAX_WEIGHT * residual / (storage + spacing * w...]
  transfers between devices with their start and end apart: 52 -> 0, of which waited for: 15 -> 0; matrix products, arithmetic and copies ran while one was open for 30% -> 0% of each run, Pallas kernels for 0% -> 0%
where the time goes in v1:
time: 46.7 us; the launch traced here: 46.4 us
  Pallas kernels  41.4 us (89%)
  local copies, waits for them, and re-layouts  4.96 us (11%)
    pallas_call x1, Pallas kernels, per_device(): pl.pallas_call(functools.partial(kernel, n_wide, n_narrow), out_shape=jax...  41.4 us
    unnamed x9, local copies, waits for them, and re-layouts  4.96 us

profile of v1, /device:TPU:23, one launch (start us, length us, event | category | flops | bytes accessed | tf_op | source)
XLA Modules:
  0.0 46.4 jit_solution(7811892146620943822)
XLA Ops:
  0.0 0.0 copy-start
  0.0 1.0 %copy-done = f32[4,64,512]{2,1,0:T(8,128)S(1)} copy-done((f32[4,64,512]{2,1,0:T(8,128)S(1)}, f32[4,64,512]{2,1,0:T(8,128)}, u32[]{:S(2)}) %copy-start) | copy-done | bytes 524312
  1.0 0.0 copy-start.1
  1.0 1.0 %copy-done.1 = f32[4,64,512]{2,1,0:T(8,128)S(1)} copy-done((f32[4,64,512]{2,1,0:T(8,128)S(1)}, f32[4,64,512]{2,1,0:T(8,128)}, u32[]{:S(2)}) %copy-start.1) | copy-done | bytes 524312
  2.1 0.0 copy-start.2
  2.1 1.0 %copy-done.2 = f32[4,64,512]{2,1,0:T(8,128)S(1)} copy-done((f32[4,64,512]{2,1,0:T(8,128)S(1)}, f32[4,64,512]{2,1,0:T(8,128)}, u32[]{:S(2)}) %copy-start.2) | copy-done | bytes 524312
  3.1 0.0 copy-start.3
  3.1 1.0 %copy-done.3 = s32[4,64,512]{2,1,0:T(8,128)S(1)} copy-done((s32[4,64,512]{2,1,0:T(8,128)S(1)}, s32[4,64,512]{2,1,0:T(8,128)}, u32[]{:S(2)}) %copy-start.3) | copy-done | bytes 524312
  4.2 41.4 %vcycle.1 = f32[4,64,512]{2,1,0:T(8,128)S(1)} custom-call(f32[4,64,512]{2,1,0:T(8,128)S(1)} %copy-done, f32[4,64,512]{2,1,0:T(8,128)S(1)} %copy-done.1, f32[4,64,512]{2,1,0:T(8,128)S(1)} %copy-done.2, s32[4,64,512]{2,1,0:T(8,128)S(1)} %copy-done.3), custom_call_target="tpu_custom_call" | custom-call | tf_op jit(solution)/shard_map/vcycle/pallas_call | solution.py:490
  45.6 0.8 %copy.6 = f32[4,64,512]{2,1,0:T(8,128)} copy(f32[4,64,512]{2,1,0:T(8,128)S(1)} %vcycle.1) | data formatting | bytes 1048576
Async XLA Ops:
  0.0 1.0 %copy-start = (f32[4,64,512]{2,1,0:T(8,128)S(1)}, f32[4,64,512]{2,1,0:T(8,128)}, u32[]{:S(2)}) copy-start(f32[4,64,512]{2,1,0:T(8,128)} %pressure.1) | copy-start | bytes 1572868
  1.0 1.0 %copy-start.1 = (f32[4,64,512]{2,1,0:T(8,128)S(1)}, f32[4,64,512]{2,1,0:T(8,128)}, u32[]{:S(2)}) copy-start(f32[4,64,512]{2,1,0:T(8,128)} %source.1) | copy-start | bytes 1572868
  2.1 1.0 %copy-start.2 = (f32[4,64,512]{2,1,0:T(8,128)S(1)}, f32[4,64,512]{2,1,0:T(8,128)}, u32[]{:S(2)}) copy-start(f32[4,64,512]{2,1,0:T(8,128)} %permeability.1) | copy-start | bytes 1572868
  3.1 1.0 %copy-start.3 = (s32[4,64,512]{2,1,0:T(8,128)S(1)}, s32[4,64,512]{2,1,0:T(8,128)}, u32[]{:S(2)}) copy-start(s32[4,64,512]{2,1,0:T(8,128)} %active_mask.1) | copy-start | bytes 1572868

commit v2 on v1

--- a/solution.py
+++ b/solution.py
@@ -65,15 +65,23 @@
         value = conduct(here, y_next(here), self.spacing)
         self.ty[plane, :, pl.ds(row, rows), :] = jnp.where(last, 0.0, value)
 
-    def make_diag(self, plane, row, rows):
+    def make_partial(self, plane, row, rows, faces):
         at, after = pl.ds(row, rows), pl.ds(row + 1, rows)
         along = self.ty[plane, :, at, :]
-        total = self.storage + self.tx[plane, :, at, :] + self.tx[plane + 1, :, at, :]
-        total = total + self.tz[plane, :, at, :] + self.tz[plane, :, after, :]
+        total = self.storage + self.tz[plane, :, at, :] + self.tz[plane, :, after, :]
         total = total + along + y_prev(along)
+        for face in faces:
+            total = total + self.tx[face, :, at, :]
+        return total
+
+    def set_diag(self, plane, row, rows, total):
+        at = pl.ds(row, rows)
         if self.diag is not None:
             self.diag[plane, :, at, :] = total
         self.inv[plane, :, at, :] = jnp.where(self.perm[plane, :, at, :] > 0.0, 0.8 / total, 0.0)
+
+    def make_diag(self, plane, row, rows):
+        self.set_diag(plane, row, rows, self.make_partial(plane, row, rows, (plane, plane + 1)))
 
     def flow(self, field, plane, row, rows):
         at, after = pl.ds(row, rows), pl.ds(row + 1, rows)
@@ -118,7 +126,7 @@
     pressure, source, permeability, active_mask, out,
     raw, act, rhs, v0, v1, v2, v3, perm, tx, tz, ty, diag, inv, resid,
     zs1, zr1, zs2, zr2, zs3, zr3,
-    m_raw, m_perm, m_tx, m_tz, m_ty, m_diag, m_inv, m_rhs, m_f1, m_f2, m_u, m_fin, m_refx, m_refz, m_res, rc, rf,
+    m_raw, m_perm, m_tx, m_tz, m_ty, m_diag, m_inv, m_rhs, m_f1, m_f2, m_u, m_fin, m_ref, m_corner, m_refz, m_res, rc, rf,
     c_perm, c_tx, c_tz, c_ty, c_inv, c_f1, c_f2, c_f3, c_f4,
     load_sem, send_sem, recv_sem,
 ):
@@ -137,39 +145,50 @@
             ok = one if ok is None else ok & one
         return ok
 
-    class Swap:
-        def __init__(self, dx, dz, src, dst):
-            slot = slots[0]
-            slots[0] += 1
-            self.ok, self.back = exists(dx, dz), exists(-dx, -dz)
-            self.copy = pltpu.make_async_remote_copy(
-                src_ref=src, dst_ref=dst, send_sem=send_sem.at[slot], recv_sem=recv_sem.at[slot],
-                device_id=(wide + dx, narrow + dz), device_id_type=MESH,
-            )
-
-        def start(self):
-            pl.when(self.ok)(self.copy.start)
-
-        def wait_recv(self):
-            pl.when(self.back)(self.copy.wait_recv)
-
-        def wait_send(self):
-            pl.when(self.ok)(self.copy.wait_send)
-
+    odd = lax.rem(wide, 2)
+    chip_step, off_step = 1 - 2 * odd, 2 * odd - 1
+    off_ok = ((odd == 1) & (wide + 1 < n_wide)) | ((odd == 0) & (wide > 0))
+    near, far = 4 - 3 * odd, 1 + 3 * odd
+    near_face, far_face = 5 - 4 * odd, 1 + 4 * odd
+    chip_at, off_at = 5 * odd, 5 - 5 * odd
+    mid_near, mid_far = 3 - odd, 2 + odd
     everyone = []
 
-    def swaps(items):
-        made = [Swap(*item) for item in items]
-        everyone.extend(made)
-        return made
+    def swap(ok, back, step_x, step_z, src, dst):
+        slot = len(everyone)
+        copy = pltpu.make_async_remote_copy(
+            src_ref=src, dst_ref=dst, send_sem=send_sem.at[slot], recv_sem=recv_sem.at[slot],
+            device_id=(wide + step_x, narrow + step_z), device_id_type=MESH,
+        )
+        everyone.append((ok, back, copy))
+        return everyone[-1]
+
+    def with_chip(src, dst, dz=0):
+        if dz == 0:
+            return swap(None, None, chip_step, 0, src, dst)
+        return swap(exists(0, dz), exists(0, -dz), chip_step, dz, src, dst)
+
+    def with_off(src, dst, dz=0):
+        if dz == 0:
+            return swap(off_ok, off_ok, off_step, 0, src, dst)
+        return swap(off_ok & exists(0, dz), off_ok & exists(0, -dz), off_step, dz, src, dst)
+
+    def with_z(dz, src, dst):
+        return swap(exists(0, dz), exists(0, -dz), 0, dz, src, dst)
+
+    def guarded(ok, act_on):
+        if ok is None:
+            act_on()
+        else:
+            pl.when(ok)(act_on)
 
     def start(group):
-        for one in group:
-            one.start()
+        for ok, _, copy in group:
+            guarded(ok, copy.start)
 
     def wait(group):
-        for one in group:
-            one.wait_recv()
+        for _, back, copy in group:
+            guarded(back, copy.wait_recv)
 
     peers = [(dx, dz) for dx in range(-REACH, REACH + 1) for dz in (-1, 0, 1) if (dx, dz) != (0, 0)]
 
@@ -185,7 +204,7 @@
             copy.start()
             loads.append(copy)
 
-    for ref in (m_perm, m_f1, m_refx, m_refz, c_perm, c_f1, zr1, zr2, zr3):
+    for ref in (m_perm, m_f1, m_ref, m_corner, m_refz, c_perm, c_f1, zr1, zr2, zr3):
         ref[...] = jnp.zeros(ref.shape, F32)
     for ref in (m_u, m_f2, c_f2, c_f3):
         ref[...] = jnp.zeros(ref.shape, F32)
@@ -233,15 +252,21 @@
                 for block in range(4):
                     field[plane + 1, block, pl.ds(row, 1), :] = buffer[side, pl.ds(plane * 4 + block, 1), :]
 
-    def fine_x(field):
+    pieces = (0, 3, 1, 2)
+
+    def fine_chip(field):
         rows = pl.ds(8, 64)
-        return swaps([
-            (-1, 0, field.at[1, :, rows, :], field.at[5, :, rows, :]),
-            (1, 0, field.at[4, :, rows, :], field.at[0, :, rows, :]),
-        ])
+        return [with_chip(field.at[near, :, rows, :], field.at[chip_at, :, rows, :])]
+
+    def fine_off(field):
+        made = {}
+        for piece in pieces:
+            rows = pl.ds(8 + 16 * piece, 16)
+            made[piece] = [with_off(field.at[far, :, rows, :], field.at[off_at, :, rows, :])]
+        return made
 
     def fine_z(send, recv):
-        return swaps([(0, -1, send.at[0], recv.at[1]), (0, 1, send.at[1], recv.at[0])])
+        return [with_z(-1, send.at[0], recv.at[1]), with_z(1, send.at[1], recv.at[0])]
 
     pack(zs1.at[0], perm)
     pack(zs1.at[1], v0)
@@ -250,10 +275,14 @@
     count_z = jnp.minimum(narrow, 1) + jnp.minimum(n_narrow - 1 - narrow, 1) + 1
     pl.semaphore_wait(barrier, count_x * count_z - 1)
 
-    perm_x, v0_x = fine_x(perm), fine_x(v0)
+    perm_chip, v0_chip = fine_chip(perm), fine_chip(v0)
+    perm_off, v0_off = fine_off(perm), fine_off(v0)
     perm_z = fine_z(zs1.at[0], zr1.at[0])
     v0_z = fine_z(zs1.at[1], zr1.at[1])
-    start(perm_x + v0_x + perm_z + v0_z)
+    start(perm_chip + v0_chip)
+    start(perm_z + v0_z)
+    for piece in pieces:
+        start(perm_off[piece] + v0_off[piece])
 
     for plane in range(2):
         for block in range(2):
@@ -265,33 +294,34 @@
     def mid_swaps(ref):
         own, low, high = pl.ds(16, 32), pl.ds(16, 8), pl.ds(40, 8)
         below, above = pl.ds(8, 8), pl.ds(48, 8)
-        two = pl.ds(2, 2)
-        return swaps([
-            (-1, 0, ref.at[two, :, own, :], ref.at[pl.ds(4, 2), :, own, :]),
-            (1, 0, ref.at[two, :, own, :], ref.at[pl.ds(0, 2), :, own, :]),
-            (0, -1, ref.at[two, :, low, :], ref.at[two, :, above, :]),
-            (0, 1, ref.at[two, :, high, :], ref.at[two, :, below, :]),
-            (-1, -1, ref.at[2, :, low, :], ref.at[4, :, above, :]),
-            (-1, 1, ref.at[2, :, high, :], ref.at[4, :, below, :]),
-            (1, -1, ref.at[3, :, low, :], ref.at[1, :, above, :]),
-            (1, 1, ref.at[3, :, high, :], ref.at[1, :, below, :]),
-        ])
+        groups = []
+        for plane in (mid_near, mid_far):
+            over, back = plane + 2 - 4 * odd, plane - 2 + 4 * odd
+            group = [
+                with_off(ref.at[plane, :, own, :], ref.at[over, :, own, :]),
+                with_chip(ref.at[plane, :, own, :], ref.at[back, :, own, :]),
+                with_z(-1, ref.at[plane, :, low, :], ref.at[plane, :, above, :]),
+                with_z(1, ref.at[plane, :, high, :], ref.at[plane, :, below, :]),
+            ]
+            cross, there = (with_chip, back) if plane is mid_near else (with_off, over)
+            group.append(cross(ref.at[plane, :, low, :], ref.at[there, :, above, :], -1))
+            group.append(cross(ref.at[plane, :, high, :], ref.at[there, :, below, :], 1))
+            groups.append(group)
+        return groups
 
     def coarse_swaps(ref):
         mine = {0: pl.ds(16, 16), -1: pl.ds(16, 8), 1: pl.ds(24, 8)}
         theirs = {0: pl.ds(16, 16), -1: pl.ds(32, 8), 1: pl.ds(8, 8)}
-        return swaps([
-            (dx, dz, ref.at[4, :, mine[dz], :], ref.at[4 - dx, :, theirs[dz], :])
+        return [
+            swap(exists(dx, dz), exists(-dx, -dz), dx, dz, ref.at[4, :, mine[dz], :], ref.at[4 - dx, :, theirs[dz], :])
             for dx, dz in sorted(peers, key=lambda one: -abs(one[0]))
-        ])
-
-    mid_perm_swaps = mid_swaps(m_perm)
-    start(mid_perm_swaps)
+        ]
+
+    mid_perm_near, mid_perm_far = mid_swaps(m_perm)
     some = coarsen(m_perm, 2, 0, 16, 16) > 0.0
     value = coarsen(m_raw, 0, 0, 0, 16) * 0.125
     c_perm[4, 0, pl.ds(16, 16), :] = jnp.where(some, value, 0.0)
     coarse_perm_swaps = coarse_swaps(c_perm)
-    start(coarse_perm_swaps)
 
     def inner(row):
         for plane in range(1, 5):
@@ -306,7 +336,24 @@
             fine.make_tz(plane, row, 8)
 
     chunks(16, 72, inner_z)
-
+    inside = (near, 2, 3)
+
+    def relax(old, new, plane, row, first):
+        at = pl.ds(row, 8)
+        here, total = fine.flow(old, plane, row, 8)
+        if first:
+            here = jnp.where(perm[plane, :, at, :] > 0.0, here, 0.0)
+        force = rhs[plane - 1, :, pl.ds(row - 8, 8), :] + total
+        new[plane, :, at, :] = 0.2 * here + inv[plane, :, at, :] * force
+
+    def residual(plane, row):
+        at = pl.ds(row, 8)
+        here, total = fine.flow(v2, plane, row, 8)
+        value = rhs[plane - 1, :, pl.ds(row - 8, 8), :] + total - diag[plane, :, at, :] * here
+        resid[plane - 1, :, pl.ds(row - 8, 8), :] = jnp.where(perm[plane, :, at, :] > 0.0, value, 0.0)
+
+    wait(perm_chip)
+    chunks(8, 72, lambda row: fine.make_tx(near_face, row, 8))
     wait(perm_z + v0_z)
     unpack(perm, zr1.at[0])
     unpack(v0, zr1.at[1])
@@ -314,43 +361,57 @@
     inner_z(72)
     for copy in loads[12:]:
         copy.wait()
-    chunks(8, 72, lambda row: [fine.make_diag(plane, row, 8) for plane in (2, 3)])
-
-    def relax(old, new, planes, first):
+
+    def inside_diag(row):
+        for plane in inside:
+            fine.make_diag(plane, row, 8)
+        diag[far, :, pl.ds(row, 8), :] = fine.make_partial(far, row, 8, (2 + 2 * odd,))
+
+    chunks(8, 72, inside_diag)
+    wait(v0_chip)
+
+    v1_chip, v1_off, v1_z = fine_chip(v1), fine_off(v1), fine_z(zs2, zr2)
+    v2_chip, v2_off, v2_z = fine_chip(v2), fine_off(v2), fine_z(zs3, zr3)
+    mid_f1_near, mid_f1_far = mid_swaps(m_f1)
+
+    def relax_inside(old, new, first, rows):
         def body(row):
-            at = pl.ds(row, 8)
-            for plane in planes:
-                here, total = fine.flow(old, plane, row, 8)
-                if first:
-                    here = jnp.where(perm[plane, :, at, :] > 0.0, here, 0.0)
-                force = rhs[plane - 1, :, pl.ds(row - 8, 8), :] + total
-                new[plane, :, at, :] = 0.2 * here + inv[plane, :, at, :] * force
-        chunks(8, 72, body)
-
-    wait(perm_x)
-
-    def outer(row):
-        fine.make_tx(1, row, 8)
-        fine.make_tx(5, row, 8)
-        fine.make_diag(1, row, 8)
-        fine.make_diag(4, row, 8)
-
-    chunks(8, 72, outer)
-    wait(v0_x)
-
-    def sweep(old, new, first, send, recv):
-        relax(old, new, (1, 4), first)
-        by_x = fine_x(new)
-        start(by_x)
-        relax(old, new, (2, 3), first)
-        pack(send, new)
-        by_z = fine_z(send, recv)
-        start(by_z)
-        return by_x, by_z
-
-    v1_x, v1_z = sweep(v0, v1, True, zs2, zr2)
-
-    wait(mid_perm_swaps)
+            for plane in inside:
+                relax(old, new, plane, row, first)
+        for low, high in rows:
+            chunks(low, high, body)
+
+    relax_inside(v0, v1, True, ((8, 72),))
+    start(v1_chip)
+    for piece in pieces:
+        wait(perm_off[piece] + v0_off[piece])
+        for row in (8 + 16 * piece, 16 + 16 * piece):
+            fine.make_tx(far_face, row, 8)
+            fine.set_diag(far, row, 8, diag[far, :, pl.ds(row, 8), :] + tx[far_face, :, pl.ds(row, 8), :])
+            relax(v0, v1, far, row, True)
+        start(v1_off[piece])
+        if piece == 3:
+            pack(zs2, v1)
+            start(v1_z)
+    start(mid_perm_near + mid_perm_far)
+
+    wait(v1_chip)
+    relax_inside(v1, v2, False, ((16, 64),))
+    wait(v1_z)
+    unpack(v1, zr2)
+    relax_inside(v1, v2, False, ((8, 16), (64, 72)))
+    start(v2_chip)
+    for piece in pieces:
+        wait(v1_off[piece])
+        for row in (8 + 16 * piece, 16 + 16 * piece):
+            relax(v1, v2, far, row, False)
+        start(v2_off[piece])
+        if piece == 3:
+            pack(zs3, v2)
+            start(v2_z)
+    start(coarse_perm_swaps)
+
+    wait(mid_perm_near + mid_perm_far)
     for plane in range(1, 6):
         mid.make_tx(plane, 8, 48)
     for plane in range(1, 5):
@@ -358,10 +419,33 @@
         mid.make_tz(plane, 8, 56)
         mid.make_diag(plane, 8, 48)
 
-    wait(v1_z)
-    unpack(v1, zr2)
-    wait(v1_x)
-    v2_x, v2_z = sweep(v1, v2, False, zs3, zr3)
+    own = pl.ds(16, 32)
+
+    def mid_first(plane):
+        for block in range(2):
+            value = coarsen(resid, 2 * (plane - 2), block, 0, 32)
+            value = jnp.where(m_perm[plane, block, own, :] > 0.0, value, 0.0)
+            m_rhs[plane - 2, block] = value
+            m_f1[plane, block, own, :] = m_inv[plane, block, own, :] * value
+
+    def inside_residual(row):
+        for plane in inside:
+            residual(plane, row)
+
+    wait(v2_chip)
+    chunks(16, 64, inside_residual)
+    wait(v2_z)
+    unpack(v2, zr3)
+    chunks(8, 16, inside_residual)
+    chunks(64, 72, inside_residual)
+    mid_first(mid_near)
+    start(mid_f1_near)
+    for piece in pieces:
+        wait(v2_off[piece])
+        for row in (8 + 16 * piece, 16 + 16 * piece):
+            residual(far, row)
+    mid_first(mid_far)
+    start(mid_f1_far)
 
     wait(coarse_perm_swaps)
     for plane in range(1, 9):
@@ -371,31 +455,7 @@
         coarse.make_tz(plane, 8, 40)
         coarse.make_diag(plane, 8, 32)
 
-    def residual(planes):
-        def body(row):
-            at = pl.ds(row, 8)
-            for plane in planes:
-                here, total = fine.flow(v2, plane, row, 8)
-                value = rhs[plane - 1, :, pl.ds(row - 8, 8), :] + total - diag[plane, :, at, :] * here
-                resid[plane - 1, :, pl.ds(row - 8, 8), :] = jnp.where(perm[plane, :, at, :] > 0.0, value, 0.0)
-        chunks(8, 72, body)
-
-    wait(v2_z)
-    unpack(v2, zr3)
-    residual((2, 3))
-    wait(v2_x)
-    residual((1, 4))
-
-    own = pl.ds(16, 32)
-    for plane in range(2):
-        for block in range(2):
-            value = coarsen(resid, 2 * plane, block, 0, 32)
-            value = jnp.where(m_perm[plane + 2, block, own, :] > 0.0, value, 0.0)
-            m_rhs[plane, block] = value
-            m_f1[plane + 2, block, own, :] = m_inv[plane + 2, block, own, :] * value
-    mid_f1_swaps = mid_swaps(m_f1)
-    start(mid_f1_swaps)
-    wait(mid_f1_swaps)
+    wait(mid_f1_near + mid_f1_far)
     for plane in range(1, 5):
         here, total = mid.flow(m_f1, plane, 8, 48)
         m_f2[plane, :, pl.ds(8, 48), :] = 1.2 * here + m_inv[plane, :, pl.ds(8, 48), :] * total
@@ -410,13 +470,17 @@
     coarse_f1_swaps = coarse_swaps(c_f1)
     start(coarse_f1_swaps)
     tall = pl.ds(8, 48)
-    two = pl.ds(2, 2)
-    mid_f2_swaps = swaps([
-        (-1, 0, m_f2.at[two, :, tall, :], m_refx.at[1]),
-        (1, 0, m_f2.at[two, :, tall, :], m_refx.at[0]),
-        (0, -1, m_f2.at[two, :, pl.ds(16, 8), :], m_refz.at[1]),
-        (0, 1, m_f2.at[two, :, pl.ds(40, 8), :], m_refz.at[0]),
-    ])
+    two, low, high = pl.ds(2, 2), pl.ds(8, 8), pl.ds(48, 8)
+    mid_f2_swaps = [
+        with_off(m_f2.at[mid_near, :, own, :], m_ref.at[1 - odd]),
+        with_off(m_f2.at[mid_far, :, low, :], m_corner.at[1 - odd, 0]),
+        with_off(m_f2.at[mid_far, :, high, :], m_corner.at[1 - odd, 1]),
+        with_chip(m_f2.at[mid_far, :, own, :], m_ref.at[odd]),
+        with_chip(m_f2.at[mid_near, :, low, :], m_corner.at[odd, 0]),
+        with_chip(m_f2.at[mid_near, :, high, :], m_corner.at[odd, 1]),
+        with_z(-1, m_f2.at[two, :, pl.ds(16, 8), :], m_refz.at[1]),
+        with_z(1, m_f2.at[two, :, pl.ds(40, 8), :], m_refz.at[0]),
+    ]
     start(mid_f2_swaps)
     wait(coarse_f1_swaps)
     body = pl.ds(8, 32)
@@ -432,14 +496,17 @@
     wait(mid_f2_swaps)
     for plane in range(6):
         for block in range(2):
+            if plane in (0, 5):
+                side = plane // 5
+                add = jnp.where(m_perm[plane, block, own, :] > 0.0, rc[plane // 2, block, own, :], 0.0)
+                m_u[plane, block, own, :] = m_ref[side, block] + add
+                continue
             add = jnp.where(m_perm[plane, block, tall, :] > 0.0, rc[plane // 2, block, tall, :], 0.0)
             if plane in (2, 3):
-                base = jnp.concatenate([
-                    m_refz[0, plane - 2, block], m_f2[plane, block, own, :], m_refz[1, plane - 2, block]
-                ], 0)
+                below, above = m_refz[0, plane - 2, block], m_refz[1, plane - 2, block]
             else:
-                base = m_refx[plane // 4, plane % 2, block]
-            m_u[plane, block, tall, :] = base + add
+                below, above = m_corner[plane // 4, 0, block], m_corner[plane // 4, 1, block]
+            m_u[plane, block, tall, :] = jnp.concatenate([below, m_f2[plane, block, own, :], above], 0) + add
     for plane in range(1, 5):
         value, total = mid.flow(m_u, plane, 8, 48)
         value = 0.2 * value + m_f1[plane, :, tall, :] + m_inv[plane, :, tall, :] * total
@@ -467,8 +534,8 @@
                 out[plane - 1, pl.ds(pl.multiple_of(row - 8, 8), 8), pl.ds(block * LANES, LANES)] = value[block]
 
     chunks(8, 72, finish)
-    for one in everyone:
-        one.wait_send()
+    for ok, _, copy in everyone:
+        guarded(ok, copy.wait_send)
 
 
 def per_device(n_wide, n_narrow, pressure, source, permeability, active_mask):
@@ -483,10 +550,10 @@
     scratch += [vmem(2, 2, 16, LANES), vmem(2, 2, 16, LANES)] + [vmem(2, 16, LANES) for _ in range(4)]
     scratch += [vmem(*mid_own)] + [vmem(*mid_pad) for _ in range(6)] + [vmem(*mid_own)]
     scratch += [vmem(*mid_pad) for _ in range(4)]
-    scratch += [vmem(2, 2, 2, 48, LANES), vmem(2, 2, 2, 8, LANES), vmem(*mid_own)]
+    scratch += [vmem(2, 2, 32, LANES), vmem(2, 2, 2, 8, LANES), vmem(2, 2, 2, 8, LANES), vmem(*mid_own)]
     scratch += [vmem(3, 2, 64, LANES), vmem(4, 4, 80, LANES)]
     scratch += [vmem(*coarse_pad) for _ in range(9)]
-    scratch += [pltpu.SemaphoreType.DMA((16,)), pltpu.SemaphoreType.DMA((96,)), pltpu.SemaphoreType.DMA((96,))]
+    scratch += [pltpu.SemaphoreType.DMA((16,)), pltpu.SemaphoreType.DMA((128,)), pltpu.SemaphoreType.DMA((128,))]
     return pl.pallas_call(
         functools.partial(kernel, n_wide, n_narrow),
         out_shape=jax.ShapeDtypeStruct(pressure.shape, F32),
@@ -494,7 +561,7 @@
         out_specs=pl.BlockSpec(memory_space=pltpu.VMEM),
         scratch_shapes=scratch,
         compiler_params=pltpu.CompilerParams(
-            collective_id=0, has_side_effects=True, vmem_limit_bytes=48 * 1024 * 1024
+            collective_id=0, has_side_effects=True, vmem_limit_bytes=67043328
         ),
         name="vcycle",
     )(pressure, source, permeability, active_mask)

time: 46.7 us -> 40.9 us (0.88)
  local copies, waits for them, and re-layouts: 4.96 us -> 1.87 us
  Pallas kernels: 41.4 us -> 38.9 us
    unnamed x9 -> x1, local copies, waits for them, and re-layouts: 4.96 us -> 1.87 us
    pallas_call x1, Pallas kernels: 41.4 us -> 38.9 us  [per_device(): pl.pallas_call(functools.partial(kernel, n_wide, n_narrow), out_shape=jax...]
where the time goes in v2:
time: 40.9 us; the launch traced here: 40.8 us
  Pallas kernels  38.9 us (95%)
  local copies, waits for them, and re-layouts  1.87 us (5%)
    pallas_call x1, Pallas kernels, per_device(): pl.pallas_call(functools.partial(kernel, n_wide, n_narrow), out_shape=jax...  38.9 us
    unnamed x1, local copies, waits for them, and re-layouts  1.87 us

profile of v2, /device:TPU:23, one launch (start us, length us, event | category | flops | bytes accessed | tf_op | source)
XLA Modules:
  0.0 40.8 jit_solution(10548014394580444803)
XLA Ops:
  0.0 38.9 %vcycle.1 = f32[4,64,512]{2,1,0:T(8,128)} custom-call(f32[4,64,512]{2,1,0:T(8,128)} %pressure.1, f32[4,64,512]{2,1,0:T(8,128)} %source.1, f32[4,64,512]{2,1,0:T(8,128)} %permeability.1, s32[4,64,512]{2,1,0:T(8,128)} %active_mask.1), custom_call_target="tpu_custom_call" | custom-call | tf_op jit(solution)/shard_map/vcycle/pallas_call | solution.py:557
  38.9 1.9 %copy.6 = f32[4,64,512]{2,1,0:T(8,128)} copy(f32[4,64,512]{2,1,0:T(8,128)} %vcycle.1) | data formatting | bytes 1048576

commit v3 on v2

--- a/solution.py
+++ b/solution.py
@@ -83,14 +83,15 @@
     def make_diag(self, plane, row, rows):
         self.set_diag(plane, row, rows, self.make_partial(plane, row, rows, (plane, plane + 1)))
 
-    def flow(self, field, plane, row, rows):
+    def flow(self, field, plane, row, rows, planes=None):
+        below, mine, above = planes or (plane - 1, plane, plane + 1)
         at, after = pl.ds(row, rows), pl.ds(row + 1, rows)
-        here = field[plane, :, at, :]
+        here = field[mine, :, at, :]
         along = self.ty[plane, :, at, :]
-        total = self.tx[plane, :, at, :] * field[plane - 1, :, at, :]
-        total = total + self.tx[plane + 1, :, at, :] * field[plane + 1, :, at, :]
-        total = total + self.tz[plane, :, at, :] * field[plane, :, pl.ds(row - 1, rows), :]
-        total = total + self.tz[plane, :, after, :] * field[plane, :, after, :]
+        total = self.tx[plane, :, at, :] * field[below, :, at, :]
+        total = total + self.tx[plane + 1, :, at, :] * field[above, :, at, :]
+        total = total + self.tz[plane, :, at, :] * field[mine, :, pl.ds(row - 1, rows), :]
+        total = total + self.tz[plane, :, after, :] * field[mine, :, after, :]
         total = total + along * y_next(here) + y_prev(along * here)
         return here, total
 
@@ -128,7 +129,7 @@
     zs1, zr1, zs2, zr2, zs3, zr3,
     m_raw, m_perm, m_tx, m_tz, m_ty, m_diag, m_inv, m_rhs, m_f1, m_f2, m_u, m_fin, m_ref, m_corner, m_refz, m_res, rc, rf,
     c_perm, c_tx, c_tz, c_ty, c_inv, c_f1, c_f2, c_f3, c_f4,
-    load_sem, send_sem, recv_sem,
+    load_sem, send_sem, recv_sem, hello,
 ):
     wide, narrow = lax.axis_index("wide"), lax.axis_index("narrow")
     fine = Level(1.0, perm, tx, tz, ty, diag, inv)
@@ -210,7 +211,7 @@
         ref[...] = jnp.zeros(ref.shape, F32)
 
     barrier = pltpu.get_barrier_semaphore()
-    for dx, dz in peers:
+    for dx, dz in ((1, 0), (-1, 0), (0, 1), (0, -1)):
         @pl.when(exists(dx, dz))
         def _():
             pl.semaphore_signal(barrier, inc=1, device_id=(wide + dx, narrow + dz), device_id_type=MESH)
@@ -252,6 +253,14 @@
                 for block in range(4):
                     field[plane + 1, block, pl.ds(row, 1), :] = buffer[side, pl.ds(plane * 4 + block, 1), :]
 
+    def greet(turn):
+        pl.semaphore_signal(
+            hello.at[turn], inc=1, device_id=(wide + chip_step, narrow), device_id_type=MESH
+        )
+
+    def greeted(turn):
+        pl.semaphore_wait(hello.at[turn], 1)
+
     pieces = (0, 3, 1, 2)
 
     def fine_chip(field):
@@ -271,9 +280,9 @@
     pack(zs1.at[0], perm)
     pack(zs1.at[1], v0)
 
-    count_x = jnp.minimum(wide, REACH) + jnp.minimum(n_wide - 1 - wide, REACH) + 1
-    count_z = jnp.minimum(narrow, 1) + jnp.minimum(n_narrow - 1 - narrow, 1) + 1
-    pl.semaphore_wait(barrier, count_x * count_z - 1)
+    count_x = jnp.minimum(wide, 1) + jnp.minimum(n_wide - 1 - wide, 1)
+    count_z = jnp.minimum(narrow, 1) + jnp.minimum(n_narrow - 1 - narrow, 1)
+    pl.semaphore_wait(barrier, count_x + count_z)
 
     perm_chip, v0_chip = fine_chip(perm), fine_chip(v0)
     perm_off, v0_off = fine_off(perm), fine_off(v0)
@@ -312,10 +321,14 @@
     def coarse_swaps(ref):
         mine = {0: pl.ds(16, 16), -1: pl.ds(16, 8), 1: pl.ds(24, 8)}
         theirs = {0: pl.ds(16, 16), -1: pl.ds(32, 8), 1: pl.ds(8, 8)}
-        return [
-            swap(exists(dx, dz), exists(-dx, -dz), dx, dz, ref.at[4, :, mine[dz], :], ref.at[4 - dx, :, theirs[dz], :])
-            for dx, dz in sorted(peers, key=lambda one: -abs(one[0]))
-        ]
+        groups = ([], [], [])
+        for dx, dz in sorted(peers, key=lambda one: -abs(one[0])):
+            one = swap(
+                exists(dx, dz), exists(-dx, -dz), dx, dz,
+                ref.at[4, :, mine[dz], :], ref.at[4 - dx, :, theirs[dz], :],
+            )
+            groups[max(abs(dx) + abs(dz), 3) - 3].append(one)
+        return groups
 
     mid_perm_near, mid_perm_far = mid_swaps(m_perm)
     some = coarsen(m_perm, 2, 0, 16, 16) > 0.0
@@ -394,6 +407,7 @@
             pack(zs2, v1)
             start(v1_z)
     start(mid_perm_near + mid_perm_far)
+    greet(0)
 
     wait(v1_chip)
     relax_inside(v1, v2, False, ((16, 64),))
@@ -401,6 +415,7 @@
     unpack(v1, zr2)
     relax_inside(v1, v2, False, ((8, 16), (64, 72)))
     start(v2_chip)
+    greeted(0)
     for piece in pieces:
         wait(v1_off[piece])
         for row in (8 + 16 * piece, 16 + 16 * piece):
@@ -409,7 +424,8 @@
         if piece == 3:
             pack(zs3, v2)
             start(v2_z)
-    start(coarse_perm_swaps)
+    start(coarse_perm_swaps[0])
+    greet(1)
 
     wait(mid_perm_near + mid_perm_far)
     for plane in range(1, 6):
@@ -445,16 +461,21 @@
         for row in (8 + 16 * piece, 16 + 16 * piece):
             residual(far, row)
     mid_first(mid_far)
+    greeted(1)
     start(mid_f1_far)
-
-    wait(coarse_perm_swaps)
-    for plane in range(1, 9):
-        coarse.make_tx(plane, 8, 32)
-    for plane in range(1, 8):
-        coarse.make_ty(plane, 8, 32)
-        coarse.make_tz(plane, 8, 40)
-        coarse.make_diag(plane, 8, 32)
-
+    start(coarse_perm_swaps[1])
+
+    def coarse_faces(group, faces, planes, diags):
+        wait(group)
+        for plane in faces:
+            coarse.make_tx(plane, 8, 32)
+        for plane in planes:
+            coarse.make_ty(plane, 8, 32)
+            coarse.make_tz(plane, 8, 40)
+        for plane in diags:
+            coarse.make_diag(plane, 8, 32)
+
+    coarse_faces(coarse_perm_swaps[0], range(3, 7), range(2, 7), range(3, 6))
     wait(mid_f1_near + mid_f1_far)
     for plane in range(1, 5):
         here, total = mid.flow(m_f1, plane, 8, 48)
@@ -468,7 +489,8 @@
     value = coarsen(m_res, 0, 0, 0, 16)
     c_f1[4, 0, here, :] = c_inv[4, 0, here, :] * value
     coarse_f1_swaps = coarse_swaps(c_f1)
-    start(coarse_f1_swaps)
+    coarse_f1_swaps = coarse_f1_swaps[2] + coarse_f1_swaps[1] + coarse_f1_swaps[0]
+    start(coarse_f1_swaps + coarse_perm_swaps[2])
     tall = pl.ds(8, 48)
     two, low, high = pl.ds(2, 2), pl.ds(8, 8), pl.ds(48, 8)
     mid_f2_swaps = [
@@ -482,7 +504,15 @@
         with_z(1, m_f2.at[two, :, pl.ds(40, 8), :], m_refz.at[0]),
     ]
     start(mid_f2_swaps)
+
+    def before_correction(row):
+        for plane in range(1, 5):
+            relax(v2, v3, plane, row, False)
+
+    chunks(8, 72, before_correction)
+    coarse_faces(coarse_perm_swaps[1], (2, 7), (1, 7), (2, 6))
     wait(coarse_f1_swaps)
+    coarse_faces(coarse_perm_swaps[2], (1, 8), (), (1, 7))
     body = pl.ds(8, 32)
     for old, new, first, last in ((c_f1, c_f2, 1, 7), (c_f2, c_f3, 2, 6), (c_f3, c_f4, 3, 5)):
         for plane in range(first, last + 1):
@@ -516,20 +546,12 @@
         for block in range(4):
             refine_rows(rf, plane, block, m_fin[plane + 1, block // 2, pl.ds(12, 40), :])
 
-    def correct(row):
-        at = pl.ds(row, 8)
-        for plane in range(6):
-            add = jnp.where(perm[plane, :, at, :] > 0.0, rf[(plane + 1) // 2, :, at, :], 0.0)
-            v3[plane, :, at, :] = v2[plane, :, at, :] + add
-
-    chunks(0, 80, correct)
-
     def finish(row):
         at = pl.ds(row, 8)
         for plane in range(1, 5):
-            value, total = fine.flow(v3, plane, row, 8)
-            force = rhs[plane - 1, :, pl.ds(row - 8, 8), :] + total
-            value = 0.2 * value + inv[plane, :, at, :] * force
+            value, total = fine.flow(rf, plane, row, 8, (plane // 2, (plane + 1) // 2, (plane + 2) // 2))
+            value = jnp.where(perm[plane, :, at, :] > 0.0, 0.2 * value, 0.0)
+            value = v3[plane, :, at, :] + value + inv[plane, :, at, :] * total
             for block in range(4):
                 out[plane - 1, pl.ds(pl.multiple_of(row - 8, 8), 8), pl.ds(block * LANES, LANES)] = value[block]
 
@@ -554,6 +576,7 @@
     scratch += [vmem(3, 2, 64, LANES), vmem(4, 4, 80, LANES)]
     scratch += [vmem(*coarse_pad) for _ in range(9)]
     scratch += [pltpu.SemaphoreType.DMA((16,)), pltpu.SemaphoreType.DMA((128,)), pltpu.SemaphoreType.DMA((128,))]
+    scratch += [pltpu.SemaphoreType.REGULAR((2,))]
     return pl.pallas_call(
         functools.partial(kernel, n_wide, n_narrow),
         out_shape=jax.ShapeDtypeStruct(pressure.shape, F32),
@@ -561,10 +584,10 @@
         out_specs=pl.BlockSpec(memory_space=pltpu.VMEM),
         scratch_shapes=scratch,
         compiler_params=pltpu.CompilerParams(
-            collective_id=0, has_side_effects=True, vmem_limit_bytes=67043328
+            collective_id=0, has_side_effects=True, vmem_limit_bytes=48000000
         ),
         name="vcycle",
-    )(pressure, source, permeability, active_mask)
+    )(*[pltpu.with_memory_space_constraint(x, pltpu.HBM) for x in (pressure, source, permeability, active_mask)])
 
 
 def solution(mesh):

time: 40.9 us -> 38 us (0.929)
  Pallas kernels: 38.9 us -> 37 us
  local copies, waits for them, and re-layouts: 1.87 us -> 0.8 us
    pallas_call x1, Pallas kernels: 38.9 us -> 37 us  [per_device(): pl.pallas_call(functools.partial(kernel, n_wide, n_narrow), out_shape=jax...]
    unnamed x1, local copies, waits for them, and re-layouts: 1.87 us -> 0.8 us
where the time goes in v3:
time: 38 us; the launch traced here: 37.8 us
  Pallas kernels  37 us (97%)
  local copies, waits for them, and re-layouts  0.8 us (2%)
    pallas_call x1, Pallas kernels, per_device(): pl.pallas_call(functools.partial(kernel, n_wide, n_narrow), out_shape=jax...  37 us
    unnamed x1, local copies, waits for them, and re-layouts  0.8 us

profile of v3, /device:TPU:23, one launch (start us, length us, event | category | flops | bytes accessed | tf_op | source)
XLA Modules:
  0.0 37.8 jit_solution(12127728051887393651)
XLA Ops:
  0.0 37.0 %vcycle.1 = f32[4,64,512]{2,1,0:T(8,128)S(1)} custom-call(f32[4,64,512]{2,1,0:T(8,128)} %pressure.1, f32[4,64,512]{2,1,0:T(8,128)} %source.1, f32[4,64,512]{2,1,0:T(8,128)} %permeability.1, s32[4,64,512]{2,1,0:T(8,128)} %active_mask.1), custom_call_target="tpu_custom_call" | custom-call | tf_op jit(solution)/shard_map/vcycle/pallas_call | solution.py:580
  37.0 0.8 %copy.6 = f32[4,64,512]{2,1,0:T(8,128)} copy(f32[4,64,512]{2,1,0:T(8,128)S(1)} %vcycle.1) | data formatting | bytes 1048576
